TPU v7x, 32 devices: a whole 2x2x4 slice. The times are simulated.
32 devices in a mesh: groups: 2 (over y), space: 4 (over z), date: 2 (over x), band: 2 (over core).
Axes of the slice: x: 2, y: 2, z: 4, core: 2. Of those that a mesh axis runs over, the one named last changes fastest.
Arguments:
- reflect: float32 [16, 8, 256, 256], P('date', 'band', ('groups', 'space')), parts along dimension 2, may hold values from -6 to 6
- kernels: float32 [3, 8, 33], P(None, 'band'), may hold values from 0.2 to 2
- strength: float32 [3, 8], P(None, 'band'), may hold values from 0.2 to 0.6
- destinations: int32 [128, 1], P(('groups', 'space')), parts along dimension 0, may hold values from 0 to 3; in each aligned block of 16 rows (0 to 15, 16 to 31, ...) at most 8 rows name the same one
- offsets: int32 [128], P(('groups', 'space')), parts along dimension 0, may hold values from 0 to 60
- counts: int32 [16, 8], P('date', ('groups', 'space')), parts along dimension 1, may hold values from 1 to 8192
- resample_rows: float32 [8, 4, 4], P(('groups', 'space')), parts along dimension 0, may hold values from -3 to 3
- resample_columns: float32 [8, 128, 128], P(('groups', 'space')), parts along dimension 0, may hold values from -0.5 to 0.5
Outputs:
- geomedian: float32 [8, 512, 128], P('band', ('groups', 'space')), parts along dimension 1
There are 2 independent parts, one for each index of `groups`. A program takes and returns all parts, laid end to end along the dimension named above; an argument that names none is the same for every part. Nothing has to cross between parts.
Inputs may be any that keep to these rules, and one draw needn't show every extreme that they name: `destinations`: in each aligned block of 16 entries (the blocks of one strip) no tile is named more than 8 times, a bound that some block reaches.
All inputs are finite; a program needn't handle non-finite values.
Results may differ from a plain program's by a relative error of at most 0.00011.
Values sent between devices are 32-bit elements; how exact they have to be, the bound alone decides.
No kernel may reach another device: no remote copies, remote signals or barrier semaphores. Data moves between devices by JAX's collectives and lax.ppermute only.
A program may use at most 128 MiB of HBM per device.

v0:
```python
import functools

import jax
import jax.numpy as jnp
from jax import lax
from jax.experimental import pallas as pl
from jax.experimental.pallas import tpu as pltpu
from jax.sharding import PartitionSpec as P


BROWS = 4
BCOLS = 128
ITERS = 4
LANES = 128
SUBLANES = 8


smooth_sq = 0.01
f32 = jnp.float32
bf16 = jnp.bfloat16


def split(x):
    high = x.astype(bf16)
    return high, (x - high.astype(f32)).astype(bf16)


def mm(a, b):
    return jnp.dot(a, b, preferred_element_type=f32)


def total(terms):
    terms = list(terms)
    while len(terms) > 1:
        terms = [a + b for a, b in zip(terms[::2], terms[1::2])] + terms[len(terms) & ~1 :]
    return terms[0]


def round_up(value, unit):
    return -(-value // unit) * unit


def vmem(count):
    return [pl.BlockSpec(memory_space=pltpu.VMEM)] * count


def hbm(count):
    return [pl.BlockSpec(memory_space=pltpu.HBM)] * count


def fetch(pairs, sem):
    copies = [pltpu.make_async_copy(src, dst, sem.at[k]) for k, (src, dst) in enumerate(pairs)]
    for copy in copies:
        copy.start()
    return copies


def params(mib):
    return pltpu.CompilerParams(vmem_limit_bytes=mib << 20)


def upright(line):
    size = line.shape[1]
    eye = lax.broadcasted_iota(jnp.int32, (size, size), 0) == lax.broadcasted_iota(
        jnp.int32, (size, size), 1
    )
    spread = jnp.broadcast_to(line, (size, size))
    return jnp.sum(jnp.where(eye, spread, 0.0), axis=1, keepdims=True)


def tables_kernel(
    target_hbm,
    start_hbm,
    rows_hbm,
    count_hbm,
    out_ref,
    counted_ref,
    target_ref,
    start_ref,
    rows_ref,
    count_ref,
    sem,
    *,
    spaces,
    strip,
    halves,
    table_lines,
):
    tables = fetch(
        zip(
            (target_hbm, start_hbm, rows_hbm, count_hbm),
            (target_ref, start_ref, rows_ref, count_ref),
        ),
        sem,
    )
    width = out_ref.shape[1]
    own = lax.axis_index("space")
    for table in tables:
        table.wait()
    blocks = target_ref.shape[1]
    rows = spaces * strip
    matrix = rows_ref[0]
    lane = lax.broadcasted_iota(jnp.int32, (BROWS, width), 1) & (BROWS - 1)
    spread = jnp.zeros((BROWS, width), f32)
    for k in range(BROWS):
        spread = jnp.where(lane == k, jnp.broadcast_to(matrix[:, k : k + 1], spread.shape), spread)
    target = upright(target_ref[...].astype(f32))
    start = target * f32(blocks * BROWS) + upright(start_ref[...].astype(f32))
    length = halves * rows
    place = lax.broadcasted_iota(jnp.int32, (blocks, length), 1)
    block = lax.broadcasted_iota(jnp.int32, (blocks, length), 0)
    first = own * strip
    shift = halves.bit_length() - 1
    low = (block & (halves - 1)) * rows + (block >> shift) * BROWS + first
    inside = (place >= low) & (place < low + BROWS)
    lines = [
        jnp.sum(jnp.where(inside, table, 0.0), axis=0, keepdims=True) for table in (start, target)
    ]
    out_ref[...] = jnp.zeros(out_ref.shape, f32)
    out_ref[0:BROWS, :] = spread
    for t, line in enumerate(lines):
        for k in range(table_lines):
            at = BROWS + t * table_lines + k
            used = min(width, length - k * width)
            out_ref[at : at + 1, 0:used] = line[:, k * width : k * width + used]
    counted_ref[...] = jnp.zeros(counted_ref.shape, f32)
    counted_ref[0:1, 0 : count_ref.shape[1]] = count_ref[...].astype(f32)


def taps_kernel(kernels_hbm, strength_hbm, line_ref, gain_ref, kernels_ref, strength_ref, sem):
    for copy in fetch(((kernels_hbm, kernels_ref), (strength_hbm, strength_ref)), sem):
        copy.wait()
    passes, bands, taps_count = kernels_ref.shape
    wide = line_ref.shape[2]
    pad = jnp.zeros((bands, LANES - taps_count), f32)
    mirror = lax.broadcasted_iota(jnp.int32, (LANES, LANES), 0) + lax.broadcasted_iota(
        jnp.int32, (LANES, LANES), 1
    )
    mirror = jnp.where(mirror == taps_count - 1, 1.0, 0.0).astype(f32)
    rest = jnp.zeros((bands, wide - LANES), f32)
    for p in range(passes):
        taps = kernels_ref[p]
        taps = taps / jnp.sum(taps, axis=1, keepdims=True)
        taps = jnp.concatenate([taps, pad], axis=1)
        strength = upright(strength_ref[p : p + 1, :])
        turned = jnp.dot(taps, mirror, precision=lax.Precision.HIGHEST)
        at = slice(p * bands, (p + 1) * bands)
        line_ref[0, at, :] = jnp.concatenate([taps * strength, rest], axis=1)
        line_ref[1, at, :] = jnp.concatenate([turned, rest], axis=1)
        gain_ref[at, :] = jnp.broadcast_to(1.0 + strength, (bands, gain_ref.shape[1]))


def banded(line, size, radius):
    wide = line.shape[1]
    spread = jnp.broadcast_to(line, (size, wide))
    return split(pltpu.roll(spread, wide - radius, 1, stride=1, stride_axis=0)[:, :size])


def correct_kernel(
    x_ref, line_ref, gain_ref, counted_ref, *refs, passes, bands, radius, table_lines
):
    spaces, per, strip, width = x_ref.shape
    table_refs, (out_ref, state) = refs[:spaces], refs[spaces:]
    rows = spaces * strip
    halves = width // BCOLS
    length = halves * rows
    own = lax.axis_index("space")

    def table(t):
        lines = []
        for k in range(table_lines):
            at = BROWS + t * table_lines + k
            used = min(width, length - k * width)
            lines.append(total(ref[at : at + 1, 0:used] for ref in table_refs))
        return jnp.concatenate(lines, axis=1)

    start, target = table(0), table(1)
    entries = jnp.zeros((BROWS, length), f32)
    for d in range(spaces):
        matrix = jnp.concatenate([table_refs[d][0:BROWS, :]] * (length // width), axis=1)
        entries = jnp.where(target == (own ^ d).astype(f32), matrix, entries)
    share = (out_ref.shape[1] - SUBLANES) // per
    map_rows = out_ref.shape[0] * share
    line = lax.broadcasted_iota(jnp.int32, (map_rows, length), 0)
    offset = line - start.astype(jnp.int32)
    placer = jnp.zeros((map_rows, length), f32)
    for i in range(BROWS):
        placer = jnp.where(offset == i, entries[i : i + 1, :], placer)
    ah, al = split(placer)
    stacked = jnp.concatenate([ah, al], axis=0)

    for step in range(passes):
        middle = []
        for slot in range(bands):
            k = step * bands + slot
            rh, rl = banded(line_ref[0, k : k + 1, :], rows, radius)
            left = jnp.concatenate([rh, rh], axis=1)
            for i in range(slot, per, bands):
                if step == 0:
                    image = jnp.concatenate([x_ref[s, i] for s in range(spaces)], axis=0)
                    state[i] = image
                else:
                    image = state[i]
                xh, xl = split(image)
                both = mm(left, jnp.concatenate([xh, xl], axis=0))
                middle.append(split(both + mm(rl, xh)))
        for slot in range(bands):
            k = step * bands + slot
            ch, cl = banded(line_ref[1, k : k + 1, :], width, radius)
            group = range(slot, per, bands)
            mine = middle[slot * len(group) : (slot + 1) * len(group)]
            high = jnp.concatenate([yh for yh, _ in mine], axis=0)
            low = jnp.concatenate([yl for _, yl in mine], axis=0)
            both = mm(jnp.concatenate([high, low], axis=0), ch)
            size = high.shape[0]
            blurred = both[:size] + both[size:] + mm(high, cl)
            gain = gain_ref[k : k + 1, :]
            for q, i in enumerate(group):
                state[i] = gain * state[i] - blurred[q * rows : (q + 1) * rows]
    for i in range(0, per, 2):
        pair = range(i, min(i + 2, per))
        z = jnp.concatenate(
            [
                jnp.concatenate(
                    [state[j, :, h * BCOLS : (h + 1) * BCOLS] for h in range(halves)], axis=0
                )
                for j in pair
            ],
            axis=1,
        )
        zh, zl = split(z)
        both = mm(stacked, zh)
        laid = both[:map_rows] + both[map_rows:] + mm(ah, zl)
        for p, j in enumerate(pair):
            at = SUBLANES + j * share
            for d in range(out_ref.shape[0]):
                out_ref[d, at : at + share, :] = laid[
                    d * share : (d + 1) * share, p * BCOLS : (p + 1) * BCOLS
                ]
    for d in range(out_ref.shape[0]):
        out_ref[d, :SUBLANES, :] = counted_ref[...]


def columns_of(block, kh, kl):
    bh, bl = split(block)
    both = mm(jnp.concatenate([bh, bl], axis=0), kh)
    size = block.shape[0]
    return both[:size] + both[size:] + mm(bh, kl)


def halve_kernel(cols_ref, kh_ref, kl_ref):
    kh_ref[...], kl_ref[...] = split(cols_ref[0])


def median_kernel(
    y_ref, kh_ref, kl_ref, *refs, spaces, dates, cores, bands, local_dates
):
    out_refs, (full_ref, weight_ref, result) = refs[:cores], refs[cores:]
    sources, per, share, width = full_ref.shape
    kh, kl = kh_ref[...], kl_ref[...]
    for s in range(sources):
        full = columns_of(y_ref[s, SUBLANES:, :], kh, kl)
        full_ref[s] = full.reshape(per, share, width)
    summed = total(y_ref[s, 0:1, :] for s in range(0, sources, cores))
    mean_count = jnp.sum(summed, axis=1, keepdims=True) / f32(spaces * dates * local_dates)
    own = lax.axis_index("space")
    for x in range(dates):
        counted = y_ref[(own * dates + x) * cores, 0:1, :]
        weight = counted / (counted + mean_count)
        for t in range(local_dates):
            weight_ref[x * local_dates + t] = jnp.broadcast_to(
                weight[:, t : t + 1], weight_ref.shape[1:]
            )
    total_bands = cores * bands
    where = [[None] * total_bands for _ in range(dates * local_dates)]
    for z in range(spaces):
        for x in range(dates):
            for c in range(cores):
                for i in range(per):
                    t, b = divmod(z * per + i, bands)
                    where[x * local_dates + t][c * bands + b] = ((z * dates + x) * cores + c, i)
    tile = weight_ref.shape[1]
    for start in range(0, share, tile):
        rows = pl.ds(start, tile)

        def load(t):
            return [full_ref[s, i, rows, :] for s, i in where[t]]

        number = [jnp.zeros((tile, width), f32)] * total_bands
        below = jnp.zeros((tile, width), f32)
        for t, _ in enumerate(where):
            w = weight_ref[t]
            below = below + w
            number = [n + w * v for n, v in zip(number, load(t))]
        estimate = [n / below for n in number]
        for _ in range(ITERS):
            number = [jnp.zeros((tile, width), f32)] * total_bands
            below = jnp.zeros((tile, width), f32)
            for t, _ in enumerate(where):
                values = load(t)
                squares = []
                for v, e in zip(values, estimate):
                    gap = v - e
                    squares.append(gap * gap)
                scaled = weight_ref[t] / jnp.sqrt(total(squares) + smooth_sq)
                below = below + scaled
                number = [n + scaled * v for n, v in zip(number, values)]
            estimate = [n / below for n in number]
        for b in range(total_bands):
            result[b // bands, b % bands, rows, :] = estimate[b]
    core = lax.axis_index("band")
    for k in range(cores):
        out_refs[k][...] = result[core ^ k]


def place_kernel(*refs, dates, cores):
    out_ref = refs[-1]
    share = refs[0].shape[1]
    x, c = lax.axis_index("date"), lax.axis_index("band")
    for dx in range(dates):
        for dc in range(cores):
            j = (x ^ dx) * cores + (c ^ dc)
            at = pl.ds(pl.multiple_of(j * share, share), share)
            out_ref[:, at, :] = refs[dx * cores + dc][...]


def across_sides(pieces, dates, cores):
    received = [pieces[0]]
    for k in range(1, dates * cores):
        pairs = [
            (x * cores + c, (x ^ (k // cores)) * cores + (c ^ (k % cores)))
            for x in range(dates)
            for c in range(cores)
        ]
        received.append(lax.ppermute(pieces[k], ("date", "band"), pairs))
    return received


def local(
    reflect, kernels, strength, destinations, offsets, counts, resample_rows, resample_columns
):
    spaces, dates, cores = (lax.axis_size(a) for a in ("space", "date", "band"))
    local_dates, bands, strip, width = reflect.shape
    passes = kernels.shape[0]
    blocks = offsets.shape[0]
    rows = spaces * strip
    halves = width // BCOLS
    length = halves * rows
    table_lines = -(-length // width)
    tile_rows = blocks * BROWS
    sources = spaces * dates * cores
    share = tile_rows // (dates * cores)
    tile = min(share, SUBLANES)
    per = local_dates * bands // spaces
    images = reflect.reshape(local_dates * bands, strip, width)
    whole = lax.all_to_all(images, "space", split_axis=0, concat_axis=0, tiled=True)

    make_tables = pl.pallas_call(
        functools.partial(
            tables_kernel, spaces=spaces, strip=strip, halves=halves, table_lines=table_lines
        ),
        out_shape=[
            jax.ShapeDtypeStruct((round_up(BROWS + 2 * table_lines, SUBLANES), width), f32),
            jax.ShapeDtypeStruct((SUBLANES, BCOLS), f32),
        ],
        in_specs=hbm(4),
        out_specs=vmem(2),
        scratch_shapes=[
            pltpu.VMEM((1, blocks), jnp.int32),
            pltpu.VMEM((1, blocks), jnp.int32),
            pltpu.VMEM((1, BROWS, BROWS), f32),
            pltpu.VMEM((1, local_dates), jnp.int32),
            pltpu.SemaphoreType.DMA((4,)),
        ],
        compiler_params=params(4),
        name="tables",
    )
    table, counted = make_tables(
        destinations.reshape(1, blocks),
        offsets.reshape(1, blocks),
        resample_rows,
        counts.reshape(1, local_dates),
    )
    tables = [table]
    for d in range(1, spaces):
        tables.append(lax.ppermute(table, "space", [(i, i ^ d) for i in range(spaces)]))

    here = bands if per % bands == 0 else per
    if here != bands:
        first_band = (lax.axis_index("space") * per) % bands
        kernels = lax.dynamic_slice_in_dim(kernels, first_band, here, axis=1)
        strength = lax.dynamic_slice_in_dim(strength, first_band, here, axis=1)
    wide = max(rows, width) + LANES
    count = passes * here
    make_lines = pl.pallas_call(
        taps_kernel,
        out_shape=[
            jax.ShapeDtypeStruct((2, count, wide), f32),
            jax.ShapeDtypeStruct((count, width), f32),
        ],
        in_specs=hbm(2),
        out_specs=vmem(2),
        scratch_shapes=[
            pltpu.VMEM(kernels.shape, f32),
            pltpu.VMEM(strength.shape, f32),
            pltpu.SemaphoreType.DMA((2,)),
        ],
        compiler_params=params(4),
        name="taps",
    )
    lines, gains = make_lines(kernels, strength)

    laid = pl.pallas_call(
        functools.partial(
            correct_kernel,
            passes=passes,
            bands=here,
            radius=kernels.shape[2] // 2,
            table_lines=table_lines,
        ),
        out_shape=jax.ShapeDtypeStruct((sources, SUBLANES + per * share, BCOLS), f32),
        in_specs=vmem(4 + spaces),
        out_specs=pl.BlockSpec(memory_space=pltpu.VMEM),
        scratch_shapes=[pltpu.VMEM((per, rows, width), f32)],
        compiler_params=params(24),
        name="correct",
    )(whole.reshape(spaces, per, strip, width), lines, gains, counted, *tables)
    pixels = lax.all_to_all(
        laid, ("space", "date", "band"), split_axis=0, concat_axis=0, tiled=True
    )

    halve = pl.pallas_call(
        halve_kernel,
        out_shape=[jax.ShapeDtypeStruct((BCOLS, BCOLS), bf16)] * 2,
        in_specs=vmem(1),
        out_specs=vmem(2),
        compiler_params=params(2),
        name="halve",
    )
    columns = halve(resample_columns)
    shares = pl.pallas_call(
        functools.partial(
            median_kernel,
            spaces=spaces,
            dates=dates,
            cores=cores,
            bands=bands,
            local_dates=local_dates,
        ),
        out_shape=[jax.ShapeDtypeStruct((bands, share, BCOLS), f32)] * cores,
        in_specs=vmem(3),
        out_specs=vmem(cores),
        scratch_shapes=[
            pltpu.VMEM((sources, per, share, BCOLS), f32),
            pltpu.VMEM((dates * local_dates, tile, BCOLS), f32),
            pltpu.VMEM((cores, bands, share, BCOLS), f32),
        ],
        compiler_params=params(12),
        name="median",
    )(pixels, *columns)

    pieces = across_sides([shares[k % cores] for k in range(dates * cores)], dates, cores)
    return pl.pallas_call(
        functools.partial(place_kernel, dates=dates, cores=cores),
        out_shape=jax.ShapeDtypeStruct((bands, tile_rows, BCOLS), f32),
        in_specs=vmem(dates * cores),
        out_specs=pl.BlockSpec(memory_space=pltpu.VMEM),
        compiler_params=params(4),
        name="place",
    )(*pieces)


def solution(mesh):
    in_specs = (
        P("date", "band", ("groups", "space"), None),
        P(None, "band", None),
        P(None, "band"),
        P(("groups", "space"), None),
        P(("groups", "space")),
        P("date", ("groups", "space")),
        P(("groups", "space"), None, None),
        P(("groups", "space"), None, None),
    )
    out_specs = P("band", ("groups", "space"), None)

    return jax.shard_map(local, mesh=mesh, in_specs=in_specs, out_specs=out_specs, check_vma=False)
```

profile of v0, /device:TPU:0, one launch (start us, length us, event | category | flops | bytes accessed | tf_op | source)
XLA Modules:
  0.0 72.6 jit_solution(12162033356679136510)
XLA Ops:
  0.0 0.0 copy-start.2
  0.0 0.0 copy-start.6
  0.0 0.0 copy-start.5
  0.0 0.0 copy-start.4
  0.0 0.0 copy-start.3
  0.0 0.0 copy-start.1
  0.0 6.5 %all-to-all-start = ((f32[32,32,256]{2,1,0:T(8,128)}), f32[32,32,256]{2,1,0:T(8,128)S(1)}, u32[]{:S(2)}, u32[]{:S(2)}) async-start(f32[32,32,256]{2,1,0:T(8,128)} %bitcast.9), calls=%async_computation | async-start | bytes 2097152 | tf_op jit(solution)/shard_map/all_to_all | solution.py:356
  6.5 0.0 copy-done.2
  6.5 0.0 copy-done.6
  6.5 0.0 copy-done.5
  6.5 0.0 copy-done.4
  6.6 0.2 tables.1
  6.7 3.9 %collective-permute-start.2 = (f32[8,256]{1,0:T(8,128)S(1)}, f32[8,256]{1,0:T(8,128)S(1)}, u32[]{:S(2)}, u32[]{:S(2)}) collective-permute-start(f32[8,256]{1,0:T(8,128)S(1)} %get-tuple-element.16.refs_0_), channel_id=1, source_target_pairs={{0,12},{4,8},{8,4},{12,0},{1,13},{5,9},{9,5},{13,1},{2,14},{6,10},... | collective-permute-start | bytes 24584 | tf_op jit(solution)/shard_map/ppermute | solution.py:386
  10.6 0.0 collective-permute-start.1
  10.6 0.6 collective-permute-start
  11.3 0.0 copy-done.3
  11.3 0.0 copy-done.1
  11.3 0.3 taps.1
  11.6 16.4 %collective-permute-done.2.refs_3_ = f32[8,256]{1,0:T(8,128)S(1)} collective-permute-done((f32[8,256]{1,0:T(8,128)S(1)}, f32[8,256]{1,0:T(8,128)S(1)}, u32[]{:S(2)}, u32[]{:S(2)}) %collective-permute-start.2) | collective-permute-done | bytes 8224 | tf_op jit(solution)/shard_map/ppermute | solution.py:386
  28.0 5.0 %collective-permute-done.1.refs_2_ = f32[8,256]{1,0:T(8,128)S(1)} collective-permute-done((f32[8,256]{1,0:T(8,128)S(1)}, f32[8,256]{1,0:T(8,128)S(1)}, u32[]{:S(2)}, u32[]{:S(2)}) %collective-permute-start.1) | collective-permute-done | bytes 8224 | tf_op jit(solution)/shard_map/ppermute | solution.py:386
  33.0 0.0 collective-permute-done.refs_1_
  33.0 0.0 all-to-all-done
  33.0 4.2 %correct.1 = f32[16,136,128]{2,1,0:T(8,128)} custom-call(f32[4,8,32,256]{3,2,1,0:T(8,128)S(1)} %bitcast.5, f32[2,12,384]{2,1,0:T(8,128)S(1)} %get-tuple-element.13.line_ref, f32[12,256]{1,0:T(8,128)S(1)} %get-tuple-element.14.gain_ref, f32[8,128]{1,0:T(8,128)S(1)} %get-tuple-element.15.counted_ref, f32[8,256]{1,0:T(8,128)S(1)} %get-tuple-element.16.refs_0_, ...), custom_call_target="tpu_custom_call" | custom-call | tf_op jit(solution)/shard_map/correct/pallas_call | solution.py:413
  37.2 0.0 copy-start
  37.2 3.9 %all-to-all-start.1 = ((f32[16,136,128]{2,1,0:T(8,128)}), f32[16,136,128]{2,1,0:T(8,128)S(1)}, u32[]{:S(2)}, u32[]{:S(2)}) async-start(f32[16,136,128]{2,1,0:T(8,128)} %correct.1), calls=%async_computation.1 | async-start | bytes 2228224 | tf_op jit(solution)/shard_map/all_to_all | solution.py:428
  41.1 0.0 copy-done
  41.1 23.9 %all-to-all-done.1.y_ref = f32[16,136,128]{2,1,0:T(8,128)S(1)} async-done(((f32[16,136,128]{2,1,0:T(8,128)}), f32[16,136,128]{2,1,0:T(8,128)S(1)}, u32[]{:S(2)}, u32[]{:S(2)}) %all-to-all-start.1) | async-done | bytes 1114144 | tf_op jit(solution)/shard_map/all_to_all | solution.py:428
  65.0 1.6 %median.1 = (f32[4,16,128]{2,1,0:T(8,128)S(1)}, f32[4,16,128]{2,1,0:T(8,128)S(1)}) custom-call(f32[16,136,128]{2,1,0:T(8,128)S(1)} %all-to-all-done.1.y_ref, bf16[128,128]{1,0:T(8,128)(2,1)S(1)} %get-tuple-element.17.kh_ref, bf16[128,128]{1,0:T(8,128)(2,1)S(1)} %get-tuple-element.18.kl_ref), custom_call_target="tpu_custom_call" | custom-call | tf_op jit(solution)/shard_map/median/pallas_call | solution.py:441
  66.7 1.9 %collective-permute-start.4 = (f32[4,16,128]{2,1,0:T(8,128)S(1)}, f32[4,16,128]{2,1,0:T(8,128)S(1)}, u32[]{:S(2)}, u32[]{:S(2)}) collective-permute-start(f32[4,16,128]{2,1,0:T(8,128)S(1)} %get-tuple-element.19.refs_0_), channel_id=1, source_target_pairs={{0,2},{1,3},{2,0},{3,1},{4,6},{5,7},{6,4},{7,5},{8,10},{9,11},{10,... | collective-permute-start | bytes 98312 | tf_op jit(solution)/shard_map/ppermute | solution.py:335
  68.6 0.7 collective-permute-start.5
  69.3 0.0 collective-permute-start.3
  69.3 1.5 %collective-permute-done.4.refs_2_ = f32[4,16,128]{2,1,0:T(8,128)S(1)} collective-permute-done((f32[4,16,128]{2,1,0:T(8,128)S(1)}, f32[4,16,128]{2,1,0:T(8,128)S(1)}, u32[]{:S(2)}, u32[]{:S(2)}) %collective-permute-start.4) | collective-permute-done | bytes 32800 | tf_op jit(solution)/shard_map/ppermute | solution.py:335
  70.8 1.1 %collective-permute-done.5.refs_3_ = f32[4,16,128]{2,1,0:T(8,128)S(1)} collective-permute-done((f32[4,16,128]{2,1,0:T(8,128)S(1)}, f32[4,16,128]{2,1,0:T(8,128)S(1)}, u32[]{:S(2)}, u32[]{:S(2)}) %collective-permute-start.5) | collective-permute-done | bytes 32800 | tf_op jit(solution)/shard_map/ppermute | solution.py:335
  71.9 0.0 collective-permute-done.3.refs_1_
  72.0 0.7 place.1
  (1 shorter events, 0.0 us)
Async XLA Ops:
  0.0 6.5 %copy-start.2 = (f32[1,4,4]{2,1,0:T(4,128)S(1)}, f32[1,4,4]{2,1,0:T(4,128)}, u32[]{:S(2)}) copy-start(f32[1,4,4]{2,1,0:T(4,128)} %rows_hbm.1) | copy-start | bytes 196
  0.0 6.5 %copy-start.6 = (s32[8,1]{0,1:T(1,128)S(1)}, s32[8,1]{0,1:T(1,128)}, u32[]{:S(2)}) copy-start(s32[8,1]{0,1:T(1,128)} %param.13) | copy-start | bytes 100
  0.0 6.5 %copy-start.5 = (s32[16]{0:T(128)S(1)}, s32[16]{0:T(128)}, u32[]{:S(2)}) copy-start(s32[16]{0:T(128)} %param.12) | copy-start | bytes 196
  0.0 6.5 %copy-start.4 = (s32[16,1]{0,1:T(1,128)S(1)}, s32[16,1]{0,1:T(1,128)}, u32[]{:S(2)}) copy-start(s32[16,1]{0,1:T(1,128)} %param.11) | copy-start | bytes 196
  0.0 11.2 %copy-start.3 = (f32[3,4]{1,0:T(4,128)S(1)}, f32[3,4]{1,0:T(4,128)}, u32[]{:S(2)}) copy-start(f32[3,4]{1,0:T(4,128)} %strength_hbm.1) | copy-start | bytes 148
  0.0 11.2 %copy-start.1 = (f32[3,4,33]{2,1,0:T(4,128)S(1)}, f32[3,4,33]{2,1,0:T(4,128)}, u32[]{:S(2)}) copy-start(f32[3,4,33]{2,1,0:T(4,128)} %kernels_hbm.1) | copy-start | bytes 4756
  0.0 32.9 %all-to-all-start = ((f32[32,32,256]{2,1,0:T(8,128)}), f32[32,32,256]{2,1,0:T(8,128)S(1)}, u32[]{:S(2)}, u32[]{:S(2)}) async-start(f32[32,32,256]{2,1,0:T(8,128)} %bitcast.9), calls=%async_computation | async-start | bytes 2097152 | tf_op jit(solution)/shard_map/all_to_all | solution.py:356
  6.7 21.3 %collective-permute-start.2 = (f32[8,256]{1,0:T(8,128)S(1)}, f32[8,256]{1,0:T(8,128)S(1)}, u32[]{:S(2)}, u32[]{:S(2)}) collective-permute-start(f32[8,256]{1,0:T(8,128)S(1)} %get-tuple-element.16.refs_0_), channel_id=1, source_target_pairs={{0,12},{4,8},{8,4},{12,0},{1,13},{5,9},{9,5},{13,1},{2,14},{6,10},... | collective-permute-start | bytes 24584 | tf_op jit(solution)/shard_map/ppermute | solution.py:386
  10.6 22.3 %collective-permute-start.1 = (f32[8,256]{1,0:T(8,128)S(1)}, f32[8,256]{1,0:T(8,128)S(1)}, u32[]{:S(2)}, u32[]{:S(2)}) collective-permute-start(f32[8,256]{1,0:T(8,128)S(1)} %get-tuple-element.16.refs_0_), channel_id=1, source_target_pairs={{0,8},{4,12},{8,0},{12,4},{1,9},{5,13},{9,1},{13,5},{2,10},{6,14},... | collective-permute-start | bytes 24584 | tf_op jit(solution)/shard_map/ppermute | solution.py:386
  10.6 22.3 %collective-permute-start = (f32[8,256]{1,0:T(8,128)S(1)}, f32[8,256]{1,0:T(8,128)S(1)}, u32[]{:S(2)}, u32[]{:S(2)}) collective-permute-start(f32[8,256]{1,0:T(8,128)S(1)} %get-tuple-element.16.refs_0_), channel_id=1, source_target_pairs={{0,4},{4,0},{8,12},{12,8},{1,5},{5,1},{9,13},{13,9},{2,6},{6,2},{1... | collective-permute-start | bytes 24584 | tf_op jit(solution)/shard_map/ppermute | solution.py:386
  37.2 3.9 %copy-start = (f32[1,128,128]{2,1,0:T(8,128)S(1)}, f32[1,128,128]{2,1,0:T(8,128)}, u32[]{:S(2)}) copy-start(f32[1,128,128]{2,1,0:T(8,128)} %cols_ref.1) | copy-start | bytes 196612
  37.2 27.8 %all-to-all-start.1 = ((f32[16,136,128]{2,1,0:T(8,128)}), f32[16,136,128]{2,1,0:T(8,128)S(1)}, u32[]{:S(2)}, u32[]{:S(2)}) async-start(f32[16,136,128]{2,1,0:T(8,128)} %correct.1), calls=%async_computation.1 | async-start | bytes 2228224 | tf_op jit(solution)/shard_map/all_to_all | solution.py:428
  66.7 4.2 %collective-permute-start.4 = (f32[4,16,128]{2,1,0:T(8,128)S(1)}, f32[4,16,128]{2,1,0:T(8,128)S(1)}, u32[]{:S(2)}, u32[]{:S(2)}) collective-permute-start(f32[4,16,128]{2,1,0:T(8,128)S(1)} %get-tuple-element.19.refs_0_), channel_id=1, source_target_pairs={{0,2},{1,3},{2,0},{3,1},{4,6},{5,7},{6,4},{7,5},{8,10},{9,11},{10,... | collective-permute-start | bytes 98312 | tf_op jit(solution)/shard_map/ppermute | solution.py:335
  68.6 3.3 %collective-permute-start.5 = (f32[4,16,128]{2,1,0:T(8,128)S(1)}, f32[4,16,128]{2,1,0:T(8,128)S(1)}, u32[]{:S(2)}, u32[]{:S(2)}) collective-permute-start(f32[4,16,128]{2,1,0:T(8,128)S(1)} %get-tuple-element.20), channel_id=1, source_target_pairs={{0,3},{1,2},{2,1},{3,0},{4,7},{5,6},{6,5},{7,4},{8,11},{9,10},{10,... | collective-permute-start | bytes 98312 | tf_op jit(solution)/shard_map/ppermute | solution.py:335
  69.3 2.7 %collective-permute-start.3 = (f32[4,16,128]{2,1,0:T(8,128)S(1)}, f32[4,16,128]{2,1,0:T(8,128)S(1)}, u32[]{:S(2)}, u32[]{:S(2)}) collective-permute-start(f32[4,16,128]{2,1,0:T(8,128)S(1)} %get-tuple-element.20), channel_id=1, source_target_pairs={{0,1},{1,0},{2,3},{3,2},{4,5},{5,4},{6,7},{7,6},{8,9},{9,8},{10,11... | collective-permute-start | bytes 98312 | tf_op jit(solution)/shard_map/ppermute | solution.py:335
where the time goes:
time: 73.8 us; the launch traced here: 72.6 us
  waiting for transfers between devices  48 us (65%)
  starting transfers between devices  17.6 us (24%)
  Pallas kernels  6.98 us (9%)
    all_to_all x1, waiting for transfers between devices, local(): lax.all_to_all(laid, ('space', 'date', 'band'), split_axis=0, concat_axis...  23.9 us
    ppermute x3, waiting for transfers between devices, local(): lax.ppermute(table, 'space', [(i, i ^ d) for i in range(spaces)])  21.4 us
    all_to_all x1, starting transfers between devices, local(): lax.all_to_all(images, 'space', split_axis=0, concat_axis=0, tiled=True)  6.51 us
    ppermute x3, starting transfers between devices, local(): lax.ppermute(table, 'space', [(i, i ^ d) for i in range(spaces)])  4.53 us
    pallas_call x1, Pallas kernels, local(): pl.pallas_call(functools.partial(correct_kernel, passes=passes, bands=her...  4.22 us
    all_to_all x1, starting transfers between devices, local(): lax.all_to_all(laid, ('space', 'date', 'band'), split_axis=0, concat_axis...  3.89 us
    ppermute x3, starting transfers between devices, across_sides(): received.append(lax.ppermute(pieces[k], ('date', 'band'), pairs))  2.64 us
    ppermute x3, waiting for transfers between devices, across_sides(): received.append(lax.ppermute(pieces[k], ('date', 'band'), pairs))  2.64 us
  transfers between devices with their start and end apart: 8, of which 5 were waited for; matrix products, arithmetic and copies ran while one was open for 0% of the time, Pallas kernels for 1%

commit v1 on v0

v1 whole, which is shorter than its diff:
```python
import functools

import jax
import jax.numpy as jnp
from jax import lax
from jax.experimental import pallas as pl
from jax.experimental.pallas import tpu as pltpu
from jax.sharding import PartitionSpec as P


BROWS = 4
BCOLS = 128
ITERS = 4
LANES = 128
SUBLANES = 8


smooth_sq = 0.01
f32 = jnp.float32
bf16 = jnp.bfloat16


def split(x):
    high = x.astype(bf16)
    return high, (x - high.astype(f32)).astype(bf16)


def mm(a, b):
    return jnp.dot(a, b, preferred_element_type=f32)


def total(terms):
    terms = list(terms)
    while len(terms) > 1:
        terms = [a + b for a, b in zip(terms[::2], terms[1::2])] + terms[len(terms) & ~1 :]
    return terms[0]


def round_up(value, unit):
    return -(-value // unit) * unit


def vmem(count):
    return [pl.BlockSpec(memory_space=pltpu.VMEM)] * count


def hbm(count):
    return [pl.BlockSpec(memory_space=pltpu.HBM)] * count


def fetch(pairs, sem):
    copies = [pltpu.make_async_copy(src, dst, sem.at[k]) for k, (src, dst) in enumerate(pairs)]
    for copy in copies:
        copy.start()
    return copies


def params(mib):
    return pltpu.CompilerParams(vmem_limit_bytes=mib << 20)


def upright(line):
    size = line.shape[1]
    eye = lax.broadcasted_iota(jnp.int32, (size, size), 0) == lax.broadcasted_iota(
        jnp.int32, (size, size), 1
    )
    spread = jnp.broadcast_to(line, (size, size))
    return jnp.sum(jnp.where(eye, spread, 0.0), axis=1, keepdims=True)


def pack_kernel(
    target_hbm,
    start_hbm,
    rows_hbm,
    images_ref,
    *refs,
    halves,
    table_lines,
):
    spaces, part, strip, width = images_ref.shape
    outs, (target_ref, start_ref, rows_ref, sem) = refs[:spaces], refs[spaces:]
    tables = fetch(
        zip(
            (target_hbm, start_hbm, rows_hbm),
            (target_ref, start_ref, rows_ref),
        ),
        sem,
    )
    own = lax.axis_index("space")
    size = part * strip
    for d in range(spaces):
        outs[d][:size, :] = images_ref[own ^ d].reshape(size, width)
    for table in tables:
        table.wait()
    blocks = target_ref.shape[1]
    rows = spaces * strip
    matrix = rows_ref[0]
    lane = lax.broadcasted_iota(jnp.int32, (BROWS, width), 1) & (BROWS - 1)
    spread = jnp.zeros((BROWS, width), f32)
    for k in range(BROWS):
        spread = jnp.where(lane == k, jnp.broadcast_to(matrix[:, k : k + 1], spread.shape), spread)
    target = upright(target_ref[...].astype(f32))
    start = target * f32(blocks * BROWS) + upright(start_ref[...].astype(f32))
    length = halves * rows
    place = lax.broadcasted_iota(jnp.int32, (blocks, length), 1)
    block = lax.broadcasted_iota(jnp.int32, (blocks, length), 0)
    first = own * strip
    shift = halves.bit_length() - 1
    low = (block & (halves - 1)) * rows + (block >> shift) * BROWS + first
    inside = (place >= low) & (place < low + BROWS)
    lines = [
        jnp.sum(jnp.where(inside, table, 0.0), axis=0, keepdims=True) for table in (start, target)
    ]
    for out in outs:
        out[size:, :] = jnp.zeros((out.shape[0] - size, width), f32)
        out[size : size + BROWS, :] = spread
        for t, line in enumerate(lines):
            for k in range(table_lines):
                at = size + BROWS + t * table_lines + k
                used = min(width, length - k * width)
                out[at : at + 1, 0:used] = line[:, k * width : k * width + used]


def taps_kernel(kernels_hbm, strength_hbm, line_ref, gain_ref, kernels_ref, strength_ref, sem):
    for copy in fetch(((kernels_hbm, kernels_ref), (strength_hbm, strength_ref)), sem):
        copy.wait()
    passes, bands, taps_count = kernels_ref.shape
    wide = line_ref.shape[2]
    pad = jnp.zeros((bands, LANES - taps_count), f32)
    mirror = lax.broadcasted_iota(jnp.int32, (LANES, LANES), 0) + lax.broadcasted_iota(
        jnp.int32, (LANES, LANES), 1
    )
    mirror = jnp.where(mirror == taps_count - 1, 1.0, 0.0).astype(f32)
    rest = jnp.zeros((bands, wide - LANES), f32)
    for p in range(passes):
        taps = kernels_ref[p]
        taps = taps / jnp.sum(taps, axis=1, keepdims=True)
        taps = jnp.concatenate([taps, pad], axis=1)
        strength = upright(strength_ref[p : p + 1, :])
        turned = jnp.dot(taps, mirror, precision=lax.Precision.HIGHEST)
        at = slice(p * bands, (p + 1) * bands)
        line_ref[0, at, :] = jnp.concatenate([taps * strength, rest], axis=1)
        line_ref[1, at, :] = jnp.concatenate([turned, rest], axis=1)
        gain_ref[at, :] = jnp.broadcast_to(1.0 + strength, (bands, gain_ref.shape[1]))


def banded(line, size, radius):
    wide = line.shape[1]
    spread = jnp.broadcast_to(line, (size, wide))
    return split(pltpu.roll(spread, wide - radius, 1, stride=1, stride_axis=0)[:, :size])


def corrections(state, line_ref, gain_ref, first, passes, bands, radius):
    part, rows, width = state.shape
    groups = [[i for i in range(part) if (first + i) % bands == slot] for slot in range(bands)]
    for step in range(passes):
        middle = {}
        for slot, group in enumerate(groups):
            if group:
                k = step * bands + slot
                rh, rl = banded(line_ref[0, k : k + 1, :], rows, radius)
                left = jnp.concatenate([rh, rh], axis=1)
            for i in group:
                xh, xl = split(state[i])
                both = mm(left, jnp.concatenate([xh, xl], axis=0))
                middle[i] = split(both + mm(rl, xh))
        for slot, group in enumerate(groups):
            if not group:
                continue
            k = step * bands + slot
            ch, cl = banded(line_ref[1, k : k + 1, :], width, radius)
            high = jnp.concatenate([middle[i][0] for i in group], axis=0)
            low = jnp.concatenate([middle[i][1] for i in group], axis=0)
            both = mm(jnp.concatenate([high, low], axis=0), ch)
            size = high.shape[0]
            blurred = both[:size] + both[size:] + mm(high, cl)
            gain = gain_ref[k : k + 1, :]
            for q, i in enumerate(group):
                state[i] = gain * state[i] - blurred[q * rows : (q + 1) * rows]


def laid_pairs(state, ah, al):
    part, _, width = state.shape
    map_rows = ah.shape[0]
    stacked = jnp.concatenate([ah, al], axis=0)
    for i in range(0, part, 2):
        pair = range(i, min(i + 2, part))
        z = jnp.concatenate(
            [
                jnp.concatenate(
                    [state[j, :, h : h + BCOLS] for h in range(0, width, BCOLS)], axis=0
                )
                for j in pair
            ],
            axis=1,
        )
        zh, zl = split(z)
        both = mm(stacked, zh)
        yield pair, both[:map_rows] + both[map_rows:] + mm(ah, zl)


def small_kernel(
    line_ref, gain_ref, count_ref, *refs, spaces, cores, passes, bands, radius, share, table_lines
):
    x_refs, (*out_refs, ah_ref, al_ref, state, laid_ref) = refs[:spaces], refs[spaces:]
    part, rows, width = state.shape
    strip = rows // spaces
    tables = part * strip
    length = width // BCOLS * rows
    own = lax.axis_index("space")
    for d in range(spaces):
        at = pl.ds(pl.multiple_of((own ^ d) * strip, strip), strip)
        for i in range(part):
            state[i, at, :] = x_refs[d][i * strip : (i + 1) * strip, :]

    def table(t):
        lines = []
        for k in range(table_lines):
            at = tables + BROWS + t * table_lines + k
            used = min(width, length - k * width)
            lines.append(total(ref[at : at + 1, 0:used] for ref in x_refs))
        return jnp.concatenate(lines, axis=1)

    start, target = table(0), table(1)
    entries = jnp.zeros((BROWS, length), f32)
    for d in range(spaces):
        matrix = x_refs[d][tables : tables + BROWS, :]
        matrix = jnp.concatenate([matrix] * (length // width), axis=1)
        entries = jnp.where(target == (own ^ d).astype(f32), matrix, entries)
    line = lax.broadcasted_iota(jnp.int32, ah_ref.shape, 0)
    offset = line - start.astype(jnp.int32)
    placer = jnp.zeros(ah_ref.shape, f32)
    for i in range(BROWS):
        placer = jnp.where(offset == i, entries[i : i + 1, :], placer)
    ah, al = split(placer)
    ah_ref[...] = ah
    al_ref[...] = al
    corrections(state, line_ref, gain_ref, 0, passes, bands, radius)
    x, c = lax.axis_index("date"), lax.axis_index("band")
    groups = laid_ref.shape[0]
    for pair, laid in laid_pairs(state, ah, al):
        for m in range(groups):
            laid_ref[m, :, : laid.shape[1]] = laid[m * share : (m + 1) * share]
        for k, out in enumerate(out_refs):
            mine = (x ^ (k // cores)) * cores + (c ^ (k % cores))
            for g in range(spaces):
                lines = laid_ref[g * (groups // spaces) + mine]
                for p, j in enumerate(pair):
                    out[g, j * share : (j + 1) * share, :] = lines[
                        :, p * BCOLS : (p + 1) * BCOLS
                    ]
    counts = count_ref[...].astype(f32)
    for out in out_refs:
        for g in range(spaces):
            out[g, part * share :, :] = jnp.zeros((SUBLANES, BCOLS), f32)
            out[g, part * share : part * share + 1, 0 : counts.shape[1]] = counts


def large_kernel(
    x_ref, line_ref, gain_ref, ah_ref, al_ref, out_ref, state, *, first, passes, bands, radius
):
    spaces, part = x_ref.shape[:2]
    for i in range(part):
        state[i] = jnp.concatenate([x_ref[s, i] for s in range(spaces)], axis=0)
    corrections(state, line_ref, gain_ref, first, passes, bands, radius)
    share = out_ref.shape[1] // part
    for pair, laid in laid_pairs(state, ah_ref[...], al_ref[...]):
        for p, j in enumerate(pair):
            for d in range(out_ref.shape[0]):
                out_ref[d, j * share : (j + 1) * share, :] = laid[
                    d * share : (d + 1) * share, p * BCOLS : (p + 1) * BCOLS
                ]


def columns_of(block, kh, kl):
    bh, bl = split(block)
    both = mm(jnp.concatenate([bh, bl], axis=0), kh)
    size = block.shape[0]
    return both[:size] + both[size:] + mm(bh, kl)


def halve_kernel(cols_ref, kh_ref, kl_ref):
    kh_ref[...], kl_ref[...] = split(cols_ref[0])


def regroup_kernel(*refs, spaces):
    groups = len(refs) - spaces
    own = lax.axis_index("space")
    for d in range(spaces):
        for k in range(groups):
            refs[groups + d][k] = refs[k][own ^ d]


def columns_kernel(
    kh_ref, kl_ref, *refs, spaces, dates, cores, local_dates
):
    y_refs, (full_ref, weight_ref) = refs[:spaces], refs[spaces:]
    sides, part, share, width = full_ref.shape[1:]
    size = part * share
    kh, kl = kh_ref[...], kl_ref[...]
    for d in range(spaces):
        block = y_refs[d][:, :size, :].reshape(sides * size, width)
        full_ref[d] = columns_of(block, kh, kl).reshape(sides, part, share, width)
    counted = [y[dx * cores, size : size + 1, :] for y in y_refs for dx in range(dates)]
    summed = jnp.sum(total(counted), axis=1, keepdims=True)
    mean_count = summed / f32(spaces * dates * local_dates)
    for dx in range(dates):
        own = y_refs[0][dx * cores, size : size + 1, :]
        weight = own / (own + mean_count)
        for t in range(local_dates):
            weight_ref[dx * local_dates + t] = jnp.broadcast_to(
                weight[:, t : t + 1], weight_ref.shape[1:]
            )


def median_kernel(
    weight_ref,
    kh_ref,
    kl_ref,
    small_ref,
    y_ref,
    *refs,
    spaces,
    dates,
    cores,
    bands,
    per,
    local_dates,
):
    out_refs, (large_ref, result) = refs[:cores], refs[cores:]
    share, width = small_ref.shape[3:]
    part = small_ref.shape[2]
    kh, kl = kh_ref[...], kl_ref[...]
    for s in range(y_ref.shape[0]):
        large_ref[s] = columns_of(y_ref[s], kh, kl).reshape(per - part, share, width)
    z, x, c = (lax.axis_index(a) for a in ("space", "date", "band"))
    across = max(1, bands // per)
    inside = max(1, per // bands)
    span = bands // across
    tile = weight_ref.shape[1]
    slots = [(dc, b) for dc in range(cores) for b in range(bands)]
    order = [
        (d, dx, t) for d in range(0, spaces, across) for dx in range(dates) for t in range(inside)
    ]
    for start in range(0, share, tile):
        rows = pl.ds(start, tile)

        def load(d, dx, t):
            values = []
            for dc, b in slots:
                far = d ^ (b // span)
                image = t * bands + b % span
                if image < part:
                    values.append(small_ref[far, dx * cores + dc, image, rows, :])
                else:
                    source = ((z ^ far) * dates + (x ^ dx)) * cores + (c ^ dc)
                    values.append(large_ref[source, image - part, rows, :])
            return values

        def weight(d, dx, t):
            return weight_ref[dx * local_dates + (z ^ d) // across * inside + t]

        number = [jnp.zeros((tile, width), f32)] * len(slots)
        below = jnp.zeros((tile, width), f32)
        for key in order:
            w = weight(*key)
            below = below + w
            number = [n + w * v for n, v in zip(number, load(*key))]
        estimate = [n / below for n in number]
        for _ in range(ITERS):
            number = [jnp.zeros((tile, width), f32)] * len(slots)
            below = jnp.zeros((tile, width), f32)
            for key in order:
                values = load(*key)
                squares = []
                for v, e in zip(values, estimate):
                    gap = v - e
                    squares.append(gap * gap)
                scaled = weight(*key) / jnp.sqrt(total(squares) + smooth_sq)
                below = below + scaled
                number = [n + scaled * v for n, v in zip(number, values)]
            estimate = [n / below for n in number]
        for (dc, b), value in zip(slots, estimate):
            if across == 1:
                out_refs[dc][b, rows, :] = value
            else:
                result[dc, ((z % across) ^ (b // span)) * span + b % span, rows, :] = value
    if across > 1:
        for dc in range(cores):
            out_refs[dc][...] = result[dc]


def place_kernel(*refs, dates, cores):
    out_ref = refs[-1]
    share = refs[0].shape[1]
    x, c = lax.axis_index("date"), lax.axis_index("band")
    for dx in range(dates):
        for dc in range(cores):
            j = (x ^ dx) * cores + (c ^ dc)
            at = pl.ds(pl.multiple_of(j * share, share), share)
            out_ref[:, at, :] = refs[dx * cores + dc][...]


def across_sides(pieces, dates, cores):
    received = [pieces[0]]
    for k in range(1, dates * cores):
        pairs = [
            (x * cores + c, (x ^ (k // cores)) * cores + (c ^ (k % cores)))
            for x in range(dates)
            for c in range(cores)
        ]
        received.append(lax.ppermute(pieces[k], ("date", "band"), pairs))
    return received


def local(
    reflect, kernels, strength, destinations, offsets, counts, resample_rows, resample_columns
):
    spaces, dates, cores = (lax.axis_size(a) for a in ("space", "date", "band"))
    local_dates, bands, strip, width = reflect.shape
    passes = kernels.shape[0]
    blocks = offsets.shape[0]
    rows = spaces * strip
    halves = width // BCOLS
    length = halves * rows
    table_lines = -(-length // width)
    tile_rows = blocks * BROWS
    sources = spaces * dates * cores
    share = tile_rows // (dates * cores)
    tile = min(share, SUBLANES)
    per = local_dates * bands // spaces
    part = max(1, per // 4)
    images = reflect.reshape(spaces, per, strip, width)
    pack = pl.pallas_call(
        functools.partial(pack_kernel, halves=halves, table_lines=table_lines),
        out_shape=[
            jax.ShapeDtypeStruct(
                (part * strip + round_up(BROWS + 2 * table_lines, SUBLANES), width), f32
            )
        ]
        * spaces,
        in_specs=hbm(3) + vmem(1),
        out_specs=vmem(spaces),
        scratch_shapes=[
            pltpu.VMEM((1, blocks), jnp.int32),
            pltpu.VMEM((1, blocks), jnp.int32),
            pltpu.VMEM((1, BROWS, BROWS), f32),
            pltpu.SemaphoreType.DMA((3,)),
        ],
        compiler_params=params(4),
        name="pack",
    )
    small = list(
        pack(
            destinations.reshape(1, blocks),
            offsets.reshape(1, blocks),
            resample_rows,
            images[:, :part],
        )
    )
    for d in range(spaces - 1, 0, -1):
        small[d] = lax.ppermute(small[d], "space", [(i, i ^ d) for i in range(spaces)])
    large = lax.all_to_all(images[:, part:], "space", split_axis=0, concat_axis=0, tiled=True)

    here = bands if per % bands == 0 else per
    if here != bands:
        first_band = (lax.axis_index("space") * per) % bands
        kernels = lax.dynamic_slice_in_dim(kernels, first_band, here, axis=1)
        strength = lax.dynamic_slice_in_dim(strength, first_band, here, axis=1)
    wide = max(rows, width) + LANES
    count = passes * here
    make_lines = pl.pallas_call(
        taps_kernel,
        out_shape=[
            jax.ShapeDtypeStruct((2, count, wide), f32),
            jax.ShapeDtypeStruct((count, width), f32),
        ],
        in_specs=hbm(2),
        out_specs=vmem(2),
        scratch_shapes=[
            pltpu.VMEM(kernels.shape, f32),
            pltpu.VMEM(strength.shape, f32),
            pltpu.SemaphoreType.DMA((2,)),
        ],
        compiler_params=params(4),
        name="taps",
    )
    lines, gains = make_lines(kernels, strength)

    settings = dict(passes=passes, bands=here, radius=kernels.shape[2] // 2)
    small_rows = part * share + SUBLANES
    correct_small = pl.pallas_call(
        functools.partial(
            small_kernel,
            spaces=spaces,
            cores=cores,
            share=share,
            table_lines=table_lines,
            **settings,
        ),
        out_shape=[jax.ShapeDtypeStruct((spaces, small_rows, BCOLS), f32)] * (dates * cores)
        + [jax.ShapeDtypeStruct((spaces * tile_rows, length), bf16)] * 2,
        in_specs=vmem(3 + spaces),
        out_specs=vmem(dates * cores + 2),
        scratch_shapes=[
            pltpu.VMEM((part, rows, width), f32),
            pltpu.VMEM((spaces * tile_rows // share, share, 2 * BCOLS), f32),
        ],
        compiler_params=params(20),
        name="correct0",
    )
    *sides, ah, al = correct_small(lines, gains, counts.reshape(1, local_dates), *small)
    sides = across_sides(sides, dates, cores)
    regroup = pl.pallas_call(
        functools.partial(regroup_kernel, spaces=spaces),
        out_shape=[jax.ShapeDtypeStruct((dates * cores, small_rows, BCOLS), f32)] * spaces,
        in_specs=vmem(dates * cores),
        out_specs=vmem(spaces),
        compiler_params=params(4),
        name="regroup",
    )
    small = list(regroup(*sides))
    for d in range(spaces - 1, 0, -1):
        small[d] = lax.ppermute(small[d], "space", [(i, i ^ d) for i in range(spaces)])

    correct_large = pl.pallas_call(
        functools.partial(large_kernel, first=part, **settings),
        out_shape=jax.ShapeDtypeStruct((sources, (per - part) * share, BCOLS), f32),
        in_specs=vmem(5),
        out_specs=pl.BlockSpec(memory_space=pltpu.VMEM),
        scratch_shapes=[pltpu.VMEM((per - part, rows, width), f32)],
        compiler_params=params(20),
        name="correct1",
    )
    laid = correct_large(large, lines, gains, ah, al)
    pixels = lax.all_to_all(
        laid, ("space", "date", "band"), split_axis=0, concat_axis=0, tiled=True
    )

    halve = pl.pallas_call(
        halve_kernel,
        out_shape=[jax.ShapeDtypeStruct((BCOLS, BCOLS), bf16)] * 2,
        in_specs=vmem(1),
        out_specs=vmem(2),
        compiler_params=params(2),
        name="halve",
    )
    columns = halve(resample_columns)
    columns_call = pl.pallas_call(
        functools.partial(
            columns_kernel, spaces=spaces, dates=dates, cores=cores, local_dates=local_dates
        ),
        out_shape=[
            jax.ShapeDtypeStruct((spaces, dates * cores, part, share, BCOLS), f32),
            jax.ShapeDtypeStruct((dates * local_dates, tile, BCOLS), f32),
        ],
        in_specs=vmem(2 + spaces),
        out_specs=vmem(2),
        compiler_params=params(8),
        name="columns",
    )
    full, weights = columns_call(*columns, *small)
    shares = pl.pallas_call(
        functools.partial(
            median_kernel,
            spaces=spaces,
            dates=dates,
            cores=cores,
            bands=bands,
            per=per,
            local_dates=local_dates,
        ),
        out_shape=[jax.ShapeDtypeStruct((bands, share, BCOLS), f32)] * cores,
        in_specs=vmem(5),
        out_specs=vmem(cores),
        scratch_shapes=[
            pltpu.VMEM((sources, per - part, share, BCOLS), f32),
            pltpu.VMEM((cores, bands, share, BCOLS), f32),
        ],
        compiler_params=params(12),
        name="median",
    )(weights, *columns, full, pixels)

    pieces = across_sides([shares[k % cores] for k in range(dates * cores)], dates, cores)
    return pl.pallas_call(
        functools.partial(place_kernel, dates=dates, cores=cores),
        out_shape=jax.ShapeDtypeStruct((bands, tile_rows, BCOLS), f32),
        in_specs=vmem(dates * cores),
        out_specs=pl.BlockSpec(memory_space=pltpu.VMEM),
        compiler_params=params(4),
        name="place",
    )(*pieces)


def solution(mesh):
    in_specs = (
        P("date", "band", ("groups", "space"), None),
        P(None, "band", None),
        P(None, "band"),
        P(("groups", "space"), None),
        P(("groups", "space")),
        P("date", ("groups", "space")),
        P(("groups", "space"), None, None),
        P(("groups", "space"), None, None),
    )
    out_specs = P("band", ("groups", "space"), None)

    return jax.shard_map(local, mesh=mesh, in_specs=in_specs, out_specs=out_specs, check_vma=False)
```

time: 73.8 us -> 77.9 us (1.056); the launches traced: 72.6 us -> 77.6 us
  waiting for transfers between devices: 48 us -> 41.6 us
  starting transfers between devices: 17.6 us -> 23.6 us
  local copies, waits for them, and re-layouts: 0.03 us -> 4.4 us
  Pallas kernels: 6.98 us -> 7.86 us
    all_to_all x1, waiting for transfers between devices: 23.9 us -> 0.01 us  [local(): lax.all_to_all(laid, ('space', 'date', 'band'), split_axis=0, concat_axis...]
    ppermute x3 -> x6, waiting for transfers between devices: 2.64 us -> 12.4 us  [across_sides(): received.append(lax.ppermute(pieces[k], ('date', 'band'), pairs))]
    ppermute x3 -> x6, waiting for transfers between devices: 21.4 us -> 29.2 us  [local(): lax.ppermute(small[d], 'space', [(i, i ^ d) for i in range(spaces)])]
    ppermute x3 -> x6, starting transfers between devices: 4.53 us -> 9.22 us  [local(): lax.ppermute(small[d], 'space', [(i, i ^ d) for i in range(spaces)])]
    slice x0 -> x2, local copies, waits for them, and re-layouts: none -> 3.07 us  [the longest x1 2.1 us: local(): images[:, part:]]
    ppermute x3 -> x6, starting transfers between devices: 2.64 us -> 4.25 us  [across_sides(): received.append(lax.ppermute(pieces[k], ('date', 'band'), pairs))]
    unnamed x14, local copies, waits for them, and re-layouts: 0.03 us -> 1.34 us
    pallas_call x2 -> x5, Pallas kernels: 4.39 us -> 5.45 us  [the longest x1 3.36 us: local(): laid = correct_large(large, lines, gains, ah, al)]
  transfers between devices with their start and end apart: 8 -> 14, of which waited for: 5 -> 8; matrix products, arithmetic and copies ran while one was open for 0% -> 1% of each run, Pallas kernels for 1% -> 3%
where the time goes in v1:
time: 77.9 us; the launch traced here: 77.6 us
  waiting for transfers between devices  41.6 us (53%)
  starting transfers between devices  23.6 us (30%)
  Pallas kernels  7.86 us (10%)
  local copies, waits for them, and re-layouts  4.4 us (6%)
    ppermute x6, waiting for transfers between devices, local(): lax.ppermute(small[d], 'space', [(i, i ^ d) for i in range(spaces)])  29.2 us
    ppermute x6, waiting for transfers between devices, across_sides(): received.append(lax.ppermute(pieces[k], ('date', 'band'), pairs))  12.4 us
    ppermute x6, starting transfers between devices, local(): lax.ppermute(small[d], 'space', [(i, i ^ d) for i in range(spaces)])  9.22 us
    all_to_all x1, starting transfers between devices, local(): lax.all_to_all(images[:, part:], 'space', split_axis=0, concat_axis=0, ti...  6.35 us
    ppermute x6, starting transfers between devices, across_sides(): received.append(lax.ppermute(pieces[k], ('date', 'band'), pairs))  4.25 us
    all_to_all x1, starting transfers between devices, local(): lax.all_to_all(laid, ('space', 'date', 'band'), split_axis=0, concat_axis...  3.77 us
    pallas_call x1, Pallas kernels, local(): laid = correct_large(large, lines, gains, ah, al)  3.36 us
    slice x1, local copies, waits for them, and re-layouts, local(): images[:, part:]  2.1 us
  transfers between devices with their start and end apart: 14, of which 8 were waited for; matrix products, arithmetic and copies ran while one was open for 1% of the time, Pallas kernels for 3%

profile of v1, /device:TPU:0, one launch (start us, length us, event | category | flops | bytes accessed | tf_op | source)
XLA Modules:
  0.0 77.6 jit_solution(16461366655353675175)
XLA Ops:
  0.0 2.1 %slice.9 = f32[4,6,32,256]{3,2,1,0:T(8,128)} slice(f32[4,8,32,256]{3,2,1,0:T(8,128)} %bitcast.7), slice={[0:4], [2:8], [0:32], [0:256]} | slice | bytes 1572864 | tf_op jit(solution)/shard_map/slice | solution.py:463
  2.1 6.3 %all-to-all-start = ((f32[4,6,32,256]{3,2,1,0:T(8,128)}), f32[4,6,32,256]{3,2,1,0:T(8,128)S(1)}, u32[]{:S(2)}, u32[]{:S(2)}) async-start(f32[4,6,32,256]{3,2,1,0:T(8,128)} %slice.9), calls=%async_computation | async-start | bytes 1572864 | tf_op jit(solution)/shard_map/all_to_all | solution.py:463
  8.4 1.0 %slice.8.images_ref = f32[4,2,32,256]{3,2,1,0:T(8,128)S(1)} slice(f32[4,8,32,256]{3,2,1,0:T(8,128)} %bitcast.8), slice={[0:4], [0:2], [0:32], [0:256]} | slice | bytes 524288 | tf_op jit(solution)/shard_map/slice | solution.py:458
  9.4 0.0 copy-start.2
  9.4 0.0 copy-start.4
  9.4 0.0 copy-start.5
  9.5 0.6 copy-done.2
  10.1 0.0 copy-done.4
  10.1 0.0 copy-done.5
  10.1 0.2 pack.1
  10.3 0.0 copy-start.3
  10.3 2.1 %collective-permute-start = (f32[72,256]{1,0:T(8,128)S(1)}, f32[72,256]{1,0:T(8,128)S(1)}, u32[]{:S(2)}, u32[]{:S(2)}) collective-permute-start(f32[72,256]{1,0:T(8,128)S(1)} %get-tuple-element.32), channel_id=1, source_target_pairs={{0,4},{4,0},{8,12},{12,8},{1,5},{5,1},{9,13},{13,9},{2,6},{6,2},{1... | collective-permute-start | bytes 221192 | tf_op jit(solution)/shard_map/ppermute | solution.py:462
  12.4 2.4 %collective-permute-start.1 = (f32[72,256]{1,0:T(8,128)S(1)}, f32[72,256]{1,0:T(8,128)S(1)}, u32[]{:S(2)}, u32[]{:S(2)}) collective-permute-start(f32[72,256]{1,0:T(8,128)S(1)} %get-tuple-element.33), channel_id=1, source_target_pairs={{0,8},{4,12},{8,0},{12,4},{1,9},{5,13},{9,1},{13,5},{2,10},{6,14},... | collective-permute-start | bytes 221192 | tf_op jit(solution)/shard_map/ppermute | solution.py:462
  14.8 0.1 collective-permute-start.2
  14.8 0.0 copy-done.1
  14.8 0.0 copy-done.3
  14.8 0.3 taps.1
  15.1 8.9 %collective-permute-done.refs_1_ = f32[72,256]{1,0:T(8,128)S(1)} collective-permute-done((f32[72,256]{1,0:T(8,128)S(1)}, f32[72,256]{1,0:T(8,128)S(1)}, u32[]{:S(2)}, u32[]{:S(2)}) %collective-permute-start) | collective-permute-done | bytes 73760 | tf_op jit(solution)/shard_map/ppermute | solution.py:462
  24.0 10.1 %collective-permute-done.1.refs_2_ = f32[72,256]{1,0:T(8,128)S(1)} collective-permute-done((f32[72,256]{1,0:T(8,128)S(1)}, f32[72,256]{1,0:T(8,128)S(1)}, u32[]{:S(2)}, u32[]{:S(2)}) %collective-permute-start.1) | collective-permute-done | bytes 73760 | tf_op jit(solution)/shard_map/ppermute | solution.py:462
  34.1 0.0 collective-permute-done.2.refs_3_
  34.1 0.7 copy-done.6
  34.7 1.6 %correct0.1 = (f32[4,40,128]{2,1,0:T(8,128)S(1)}, f32[4,40,128]{2,1,0:T(8,128)S(1)}, f32[4,40,128]{2,1,0:T(8,128)S(1)}, f32[4,40,128]{2,1,0:T(8,128)S(1)}, bf16[...) custom-call(f32[2,12,384]{2,1,0:T(8,128)S(1)} %get-tuple-element.29.line_ref, ...), custom_call_target="tpu_custom_call" | custom-call | tf_op jit(solution)/shard_map/correct0/pallas_call | solution.py:512
  36.4 0.0 all-to-all-done.x_ref
  36.4 3.4 %correct1.1 = f32[16,96,128]{2,1,0:T(8,128)} custom-call(f32[4,6,32,256]{3,2,1,0:T(8,128)S(1)} %all-to-all-done.x_ref, f32[2,12,384]{2,1,0:T(8,128)S(1)} %get-tuple-element.29.line_ref, f32[12,256]{1,0:T(8,128)S(1)} %get-tuple-element.30.gain_ref, bf16[256,256]{1,0:T(8,128)(2,1)S(1)} %get-tuple-element.45.ah_ref, bf16[256,256]{1,0:T(8,128)(2,1)S(1)} %get-tuple-element.46.al_ref), custom_call_target="tpu_custom_call" | custom-call | tf_op jit(solution)/shard_map/correct1/pallas_call | solution.py:535
  39.8 3.8 %all-to-all-start.1 = ((f32[16,96,128]{2,1,0:T(8,128)}), f32[16,96,128]{2,1,0:T(8,128)S(1)}, u32[]{:S(2)}, u32[]{:S(2)}) async-start(f32[16,96,128]{2,1,0:T(8,128)} %correct1.1), calls=%async_computation.1 | async-start | bytes 1572864 | tf_op jit(solution)/shard_map/all_to_all | solution.py:536
  43.6 0.4 collective-permute-start.3
  44.0 1.6 %collective-permute-start.4 = (f32[4,40,128]{2,1,0:T(8,128)S(1)}, f32[4,40,128]{2,1,0:T(8,128)S(1)}, u32[]{:S(2)}, u32[]{:S(2)}) collective-permute-start(f32[4,40,128]{2,1,0:T(8,128)S(1)} %get-tuple-element.37), channel_id=1, source_target_pairs={{0,2},{1,3},{2,0},{3,1},{4,6},{5,7},{6,4},{7,5},{8,10},{9,11},{10,... | collective-permute-start | bytes 245768 | tf_op jit(solution)/shard_map/ppermute | solution.py:412
  45.6 0.0 collective-permute-start.5
  45.6 0.0 collective-permute-done.3.refs_1_
  45.6 8.5 %collective-permute-done.4.refs_2_ = f32[4,40,128]{2,1,0:T(8,128)S(1)} collective-permute-done((f32[4,40,128]{2,1,0:T(8,128)S(1)}, f32[4,40,128]{2,1,0:T(8,128)S(1)}, u32[]{:S(2)}, u32[]{:S(2)}) %collective-permute-start.4) | collective-permute-done | bytes 81952 | tf_op jit(solution)/shard_map/ppermute | solution.py:412
  54.1 1.2 %collective-permute-done.5.refs_3_ = f32[4,40,128]{2,1,0:T(8,128)S(1)} collective-permute-done((f32[4,40,128]{2,1,0:T(8,128)S(1)}, f32[4,40,128]{2,1,0:T(8,128)S(1)}, u32[]{:S(2)}, u32[]{:S(2)}) %collective-permute-start.5) | collective-permute-done | bytes 81952 | tf_op jit(solution)/shard_map/ppermute | solution.py:412
  55.4 0.7 collective-permute-start.6
  56.1 4.0 %collective-permute-start.7 = (f32[4,40,128]{2,1,0:T(8,128)S(1)}, f32[4,40,128]{2,1,0:T(8,128)S(1)}, u32[]{:S(2)}, u32[]{:S(2)}) collective-permute-start(f32[4,40,128]{2,1,0:T(8,128)S(1)} %get-tuple-element.41), channel_id=1, source_target_pairs={{0,8},{4,12},{8,0},{12,4},{1,9},{5,13},{9,1},{13,5},{2,10},{6,14},... | collective-permute-start | bytes 245768 | tf_op jit(solution)/shard_map/ppermute | solution.py:524
  60.1 0.0 collective-permute-start.8
  60.1 0.0 copy-done
  60.1 2.6 %collective-permute-done.6.refs_1_ = f32[4,40,128]{2,1,0:T(8,128)S(1)} collective-permute-done((f32[4,40,128]{2,1,0:T(8,128)S(1)}, f32[4,40,128]{2,1,0:T(8,128)S(1)}, u32[]{:S(2)}, u32[]{:S(2)}) %collective-permute-start.6) | collective-permute-done | bytes 81952 | tf_op jit(solution)/shard_map/ppermute | solution.py:524
  62.7 7.6 %collective-permute-done.7.refs_2_ = f32[4,40,128]{2,1,0:T(8,128)S(1)} collective-permute-done((f32[4,40,128]{2,1,0:T(8,128)S(1)}, f32[4,40,128]{2,1,0:T(8,128)S(1)}, u32[]{:S(2)}, u32[]{:S(2)}) %collective-permute-start.7) | collective-permute-done | bytes 81952 | tf_op jit(solution)/shard_map/ppermute | solution.py:524
  70.3 0.0 collective-permute-done.8.refs_3_
  70.3 0.3 columns.1
  70.6 0.0 all-to-all-done.1.y_ref
  70.6 1.4 %median.1 = (f32[4,16,128]{2,1,0:T(8,128)S(1)}, f32[4,16,128]{2,1,0:T(8,128)S(1)}) custom-call(f32[16,8,128]{2,1,0:T(8,128)S(1)} %get-tuple-element.43.weight_ref, bf16[128,128]{1,0:T(8,128)(2,1)S(1)} %get-tuple-element.27.kh_ref, bf16[128,128]{1,0:T(8,128)(2,1)S(1)} %get-tuple-element.28.kl_ref, f32[4,4,2,16,128]{4,3,2,1,0:T(8,128)S(1)} %get-tuple-element.44.small_ref, ...), custom_call_target="tpu_custom_call" | custom-call | tf_op jit(solution)/shard_map/median/pallas_call | solution.py:563
  72.0 1.5 %collective-permute-start.10 = (f32[4,16,128]{2,1,0:T(8,128)S(1)}, f32[4,16,128]{2,1,0:T(8,128)S(1)}, u32[]{:S(2)}, u32[]{:S(2)}) collective-permute-start(f32[4,16,128]{2,1,0:T(8,128)S(1)} %get-tuple-element.47.refs_0_), channel_id=1, source_target_pairs={{0,2},{1,3},{2,0},{3,1},{4,6},{5,7},{6,4},{7,5},{8,10},{9,11},{10,... | collective-permute-start | bytes 98312 | tf_op jit(solution)/shard_map/ppermute | solution.py:412
  73.6 0.0 collective-permute-start.11
  73.6 0.7 collective-permute-start.9
  74.3 1.8 %collective-permute-done.10.refs_2_ = f32[4,16,128]{2,1,0:T(8,128)S(1)} collective-permute-done((f32[4,16,128]{2,1,0:T(8,128)S(1)}, f32[4,16,128]{2,1,0:T(8,128)S(1)}, u32[]{:S(2)}, u32[]{:S(2)}) %collective-permute-start.10) | collective-permute-done | bytes 32800 | tf_op jit(solution)/shard_map/ppermute | solution.py:412
  76.0 0.9 %collective-permute-done.11.refs_3_ = f32[4,16,128]{2,1,0:T(8,128)S(1)} collective-permute-done((f32[4,16,128]{2,1,0:T(8,128)S(1)}, f32[4,16,128]{2,1,0:T(8,128)S(1)}, u32[]{:S(2)}, u32[]{:S(2)}) %collective-permute-start.11) | collective-permute-done | bytes 32800 | tf_op jit(solution)/shard_map/ppermute | solution.py:412
  76.9 0.0 collective-permute-done.9.refs_1_
  76.9 0.7 place.1
  (5 shorter events, 0.0 us)
Async XLA Ops:
  2.1 34.3 %all-to-all-start = ((f32[4,6,32,256]{3,2,1,0:T(8,128)}), f32[4,6,32,256]{3,2,1,0:T(8,128)S(1)}, u32[]{:S(2)}, u32[]{:S(2)}) async-start(f32[4,6,32,256]{3,2,1,0:T(8,128)} %slice.9), calls=%async_computation | async-start | bytes 1572864 | tf_op jit(solution)/shard_map/all_to_all | solution.py:463
  9.4 0.7 copy-start.2
  9.4 0.7 copy-start.4
  9.4 0.7 copy-start.5
  10.1 4.7 %copy-start.1 = (f32[3,4,33]{2,1,0:T(4,128)S(1)}, f32[3,4,33]{2,1,0:T(4,128)}, u32[]{:S(2)}) copy-start(f32[3,4,33]{2,1,0:T(4,128)} %kernels_hbm.1) | copy-start | bytes 4756
  10.3 4.5 %copy-start.3 = (f32[3,4]{1,0:T(4,128)S(1)}, f32[3,4]{1,0:T(4,128)}, u32[]{:S(2)}) copy-start(f32[3,4]{1,0:T(4,128)} %strength_hbm.1) | copy-start | bytes 148
  10.3 13.7 %collective-permute-start = (f32[72,256]{1,0:T(8,128)S(1)}, f32[72,256]{1,0:T(8,128)S(1)}, u32[]{:S(2)}, u32[]{:S(2)}) collective-permute-start(f32[72,256]{1,0:T(8,128)S(1)} %get-tuple-element.32), channel_id=1, source_target_pairs={{0,4},{4,0},{8,12},{12,8},{1,5},{5,1},{9,13},{13,9},{2,6},{6,2},{1... | collective-permute-start | bytes 221192 | tf_op jit(solution)/shard_map/ppermute | solution.py:462
  12.4 21.7 %collective-permute-start.1 = (f32[72,256]{1,0:T(8,128)S(1)}, f32[72,256]{1,0:T(8,128)S(1)}, u32[]{:S(2)}, u32[]{:S(2)}) collective-permute-start(f32[72,256]{1,0:T(8,128)S(1)} %get-tuple-element.33), channel_id=1, source_target_pairs={{0,8},{4,12},{8,0},{12,4},{1,9},{5,13},{9,1},{13,5},{2,10},{6,14},... | collective-permute-start | bytes 221192 | tf_op jit(solution)/shard_map/ppermute | solution.py:462
  14.8 19.3 %collective-permute-start.2 = (f32[72,256]{1,0:T(8,128)S(1)}, f32[72,256]{1,0:T(8,128)S(1)}, u32[]{:S(2)}, u32[]{:S(2)}) collective-permute-start(f32[72,256]{1,0:T(8,128)S(1)} %get-tuple-element.34), channel_id=1, source_target_pairs={{0,12},{4,8},{8,4},{12,0},{1,13},{5,9},{9,5},{13,1},{2,14},{6,10},... | collective-permute-start | bytes 221192 | tf_op jit(solution)/shard_map/ppermute | solution.py:462
  34.1 0.7 copy-start.6
  39.8 30.8 %all-to-all-start.1 = ((f32[16,96,128]{2,1,0:T(8,128)}), f32[16,96,128]{2,1,0:T(8,128)S(1)}, u32[]{:S(2)}, u32[]{:S(2)}) async-start(f32[16,96,128]{2,1,0:T(8,128)} %correct1.1), calls=%async_computation.1 | async-start | bytes 1572864 | tf_op jit(solution)/shard_map/all_to_all | solution.py:536
  43.6 2.0 %collective-permute-start.3 = (f32[4,40,128]{2,1,0:T(8,128)S(1)}, f32[4,40,128]{2,1,0:T(8,128)S(1)}, u32[]{:S(2)}, u32[]{:S(2)}) collective-permute-start(f32[4,40,128]{2,1,0:T(8,128)S(1)} %get-tuple-element.36), channel_id=1, source_target_pairs={{0,1},{1,0},{2,3},{3,2},{4,5},{5,4},{6,7},{7,6},{8,9},{9,8},{10,11... | collective-permute-start | bytes 245768 | tf_op jit(solution)/shard_map/ppermute | solution.py:412
  44.0 10.2 %collective-permute-start.4 = (f32[4,40,128]{2,1,0:T(8,128)S(1)}, f32[4,40,128]{2,1,0:T(8,128)S(1)}, u32[]{:S(2)}, u32[]{:S(2)}) collective-permute-start(f32[4,40,128]{2,1,0:T(8,128)S(1)} %get-tuple-element.37), channel_id=1, source_target_pairs={{0,2},{1,3},{2,0},{3,1},{4,6},{5,7},{6,4},{7,5},{8,10},{9,11},{10,... | collective-permute-start | bytes 245768 | tf_op jit(solution)/shard_map/ppermute | solution.py:412
  45.6 9.8 %collective-permute-start.5 = (f32[4,40,128]{2,1,0:T(8,128)S(1)}, f32[4,40,128]{2,1,0:T(8,128)S(1)}, u32[]{:S(2)}, u32[]{:S(2)}) collective-permute-start(f32[4,40,128]{2,1,0:T(8,128)S(1)} %get-tuple-element.38), channel_id=1, source_target_pairs={{0,3},{1,2},{2,1},{3,0},{4,7},{5,6},{6,5},{7,4},{8,11},{9,10},{10,... | collective-permute-start | bytes 245768 | tf_op jit(solution)/shard_map/ppermute | solution.py:412
  55.4 4.7 %copy-start = (f32[1,128,128]{2,1,0:T(8,128)S(1)}, f32[1,128,128]{2,1,0:T(8,128)}, u32[]{:S(2)}) copy-start(f32[1,128,128]{2,1,0:T(8,128)} %cols_ref.1) | copy-start | bytes 196612
  55.4 7.3 %collective-permute-start.6 = (f32[4,40,128]{2,1,0:T(8,128)S(1)}, f32[4,40,128]{2,1,0:T(8,128)S(1)}, u32[]{:S(2)}, u32[]{:S(2)}) collective-permute-start(f32[4,40,128]{2,1,0:T(8,128)S(1)} %get-tuple-element.40), channel_id=1, source_target_pairs={{0,4},{4,0},{8,12},{12,8},{1,5},{5,1},{9,13},{13,9},{2,6},{6,2},{1... | collective-permute-start | bytes 245768 | tf_op jit(solution)/shard_map/ppermute | solution.py:524
  56.1 14.2 %collective-permute-start.7 = (f32[4,40,128]{2,1,0:T(8,128)S(1)}, f32[4,40,128]{2,1,0:T(8,128)S(1)}, u32[]{:S(2)}, u32[]{:S(2)}) collective-permute-start(f32[4,40,128]{2,1,0:T(8,128)S(1)} %get-tuple-element.41), channel_id=1, source_target_pairs={{0,8},{4,12},{8,0},{12,4},{1,9},{5,13},{9,1},{13,5},{2,10},{6,14},... | collective-permute-start | bytes 245768 | tf_op jit(solution)/shard_map/ppermute | solution.py:524
  60.1 10.2 %collective-permute-start.8 = (f32[4,40,128]{2,1,0:T(8,128)S(1)}, f32[4,40,128]{2,1,0:T(8,128)S(1)}, u32[]{:S(2)}, u32[]{:S(2)}) collective-permute-start(f32[4,40,128]{2,1,0:T(8,128)S(1)} %get-tuple-element.42), channel_id=1, source_target_pairs={{0,12},{4,8},{8,4},{12,0},{1,13},{5,9},{9,5},{13,1},{2,14},{6,10},... | collective-permute-start | bytes 245768 | tf_op jit(solution)/shard_map/ppermute | solution.py:524
  72.0 4.0 %collective-permute-start.10 = (f32[4,16,128]{2,1,0:T(8,128)S(1)}, f32[4,16,128]{2,1,0:T(8,128)S(1)}, u32[]{:S(2)}, u32[]{:S(2)}) collective-permute-start(f32[4,16,128]{2,1,0:T(8,128)S(1)} %get-tuple-element.47.refs_0_), channel_id=1, source_target_pairs={{0,2},{1,3},{2,0},{3,1},{4,6},{5,7},{6,4},{7,5},{8,10},{9,11},{10,... | collective-permute-start | bytes 98312 | tf_op jit(solution)/shard_map/ppermute | solution.py:412
  73.6 3.3 %collective-permute-start.11 = (f32[4,16,128]{2,1,0:T(8,128)S(1)}, f32[4,16,128]{2,1,0:T(8,128)S(1)}, u32[]{:S(2)}, u32[]{:S(2)}) collective-permute-start(f32[4,16,128]{2,1,0:T(8,128)S(1)} %get-tuple-element.48), channel_id=1, source_target_pairs={{0,3},{1,2},{2,1},{3,0},{4,7},{5,6},{6,5},{7,4},{8,11},{9,10},{10,... | collective-permute-start | bytes 98312 | tf_op jit(solution)/shard_map/ppermute | solution.py:412
  73.6 3.3 %collective-permute-start.9 = (f32[4,16,128]{2,1,0:T(8,128)S(1)}, f32[4,16,128]{2,1,0:T(8,128)S(1)}, u32[]{:S(2)}, u32[]{:S(2)}) collective-permute-start(f32[4,16,128]{2,1,0:T(8,128)S(1)} %get-tuple-element.48), channel_id=1, source_target_pairs={{0,1},{1,0},{2,3},{3,2},{4,5},{5,4},{6,7},{7,6},{8,9},{9,8},{10,11... | collective-permute-start | bytes 98312 | tf_op jit(solution)/shard_map/ppermute | solution.py:412

commit v2 on v1

--- a/solution.py
+++ b/solution.py
@@ -74,10 +74,11 @@
     rows_hbm,
     images_ref,
     *refs,
+    part,
     halves,
     table_lines,
 ):
-    spaces, part, strip, width = images_ref.shape
+    spaces, _, strip, width = images_ref.shape
     outs, (target_ref, start_ref, rows_ref, sem) = refs[:spaces], refs[spaces:]
     tables = fetch(
         zip(
@@ -89,7 +90,7 @@
     own = lax.axis_index("space")
     size = part * strip
     for d in range(spaces):
-        outs[d][:size, :] = images_ref[own ^ d].reshape(size, width)
+        outs[d][:size, :] = images_ref[own ^ d, 0:part].reshape(size, width)
     for table in tables:
         table.wait()
     blocks = target_ref.shape[1]
@@ -119,6 +120,12 @@
                 at = size + BROWS + t * table_lines + k
                 used = min(width, length - k * width)
                 out[at : at + 1, 0:used] = line[:, k * width : k * width + used]
+
+
+def cut_kernel(images_ref, out_ref):
+    part = images_ref.shape[1] - out_ref.shape[1]
+    for s in range(out_ref.shape[0]):
+        out_ref[s] = images_ref[s, part:]
 
 
 def taps_kernel(kernels_hbm, strength_hbm, line_ref, gain_ref, kernels_ref, strength_ref, sem):
@@ -429,10 +436,10 @@
     share = tile_rows // (dates * cores)
     tile = min(share, SUBLANES)
     per = local_dates * bands // spaces
-    part = max(1, per // 4)
+    part = max(1, per // 2)
     images = reflect.reshape(spaces, per, strip, width)
     pack = pl.pallas_call(
-        functools.partial(pack_kernel, halves=halves, table_lines=table_lines),
+        functools.partial(pack_kernel, part=part, halves=halves, table_lines=table_lines),
         out_shape=[
             jax.ShapeDtypeStruct(
                 (part * strip + round_up(BROWS + 2 * table_lines, SUBLANES), width), f32
@@ -455,12 +462,21 @@
             destinations.reshape(1, blocks),
             offsets.reshape(1, blocks),
             resample_rows,
-            images[:, :part],
+            images,
         )
     )
     for d in range(spaces - 1, 0, -1):
         small[d] = lax.ppermute(small[d], "space", [(i, i ^ d) for i in range(spaces)])
-    large = lax.all_to_all(images[:, part:], "space", split_axis=0, concat_axis=0, tiled=True)
+    cut = pl.pallas_call(
+        cut_kernel,
+        out_shape=jax.ShapeDtypeStruct((spaces, per - part, strip, width), f32),
+        in_specs=vmem(1),
+        out_specs=pl.BlockSpec(memory_space=pltpu.VMEM),
+        compiler_params=params(4),
+        name="cut",
+    )
+    rest = cut(images)
+    large = lax.all_to_all(rest, "space", split_axis=0, concat_axis=0, tiled=True)
 
     here = bands if per % bands == 0 else per
     if here != bands:

time: 77.9 us -> 80.4 us (1.032)
  waiting for transfers between devices: 41.6 us -> 43.9 us
  local copies, waits for them, and re-layouts: 4.4 us -> 2.57 us
    slice x2 -> x0, local copies, waits for them, and re-layouts: 3.07 us -> none  [the longest x1 2.1 us: local(): images[:, part:]]
    ppermute x6, waiting for transfers between devices: 12.4 us -> 14.4 us  [across_sides(): received.append(lax.ppermute(pieces[k], ('date', 'band'), pairs))]
    unnamed x14 -> x18, local copies, waits for them, and re-layouts: 1.34 us -> 2.57 us
    all_to_all x1, starting transfers between devices: 3.77 us -> 4.86 us  [local(): lax.all_to_all(laid, ('space', 'date', 'band'), split_axis=0, concat_axis...]
    pallas_call x0 -> x1, Pallas kernels: none -> 0.84 us  [local(): rest = cut(images)]
  transfers between devices with their start and end apart: 14 -> 14, of which waited for: 8 -> 7; matrix products, arithmetic and copies ran while one was open for 1% -> 0% of each run, Pallas kernels for 3% -> 4%
where the time goes in v2:
time: 80.4 us; the launch traced here: 79.7 us
  waiting for transfers between devices  43.9 us (55%)
  starting transfers between devices  24.4 us (30%)
  Pallas kernels  8.62 us (11%)
  local copies, waits for them, and re-layouts  2.57 us (3%)
    ppermute x6, waiting for transfers between devices, local(): lax.ppermute(small[d], 'space', [(i, i ^ d) for i in range(spaces)])  29.6 us
    ppermute x6, waiting for transfers between devices, across_sides(): received.append(lax.ppermute(pieces[k], ('date', 'band'), pairs))  14.4 us
    ppermute x6, starting transfers between devices, local(): lax.ppermute(small[d], 'space', [(i, i ^ d) for i in range(spaces)])  8.98 us
    all_to_all x1, starting transfers between devices, local(): lax.all_to_all(rest, 'space', split_axis=0, concat_axis=0, tiled=True)  6.35 us
    all_to_all x1, starting transfers between devices, local(): lax.all_to_all(laid, ('space', 'date', 'band'), split_axis=0, concat_axis...  4.86 us
    ppermute x6, starting transfers between devices, across_sides(): received.append(lax.ppermute(pieces[k], ('date', 'band'), pairs))  4.25 us
    pallas_call x1, Pallas kernels, local(): laid = correct_large(large, lines, gains, ah, al)  2.77 us
    unnamed x18, local copies, waits for them, and re-layouts  2.57 us
  transfers between devices with their start and end apart: 14, of which 7 were waited for; matrix products, arithmetic and copies ran while one was open for 0% of the time, Pallas kernels for 4%

profile of v2, /device:TPU:0, one launch (start us, length us, event | category | flops | bytes accessed | tf_op | source)
XLA Modules:
  0.0 79.7 jit_solution(14511040663942906904)
XLA Ops:
  0.0 0.0 copy-start
  0.0 1.2 %copy-done = f32[8,4,32,256]{3,2,1,0:T(8,128)S(1)} copy-done((f32[8,4,32,256]{3,2,1,0:T(8,128)S(1)}, f32[8,4,32,256]{3,2,1,0:T(8,128)}, u32[]{:S(2)}) %copy-start) | copy-done | bytes 1048600
  1.2 0.0 copy-start.1
  1.2 0.8 %cut.1 = f32[4,4,32,256]{3,2,1,0:T(8,128)} custom-call(f32[4,8,32,256]{3,2,1,0:T(8,128)S(1)} %bitcast.4), custom_call_target="tpu_custom_call" | custom-call | tf_op jit(solution)/shard_map/cut/pallas_call | solution.py:478
  2.1 6.3 %all-to-all-start = ((f32[4,4,32,256]{3,2,1,0:T(8,128)}), f32[4,4,32,256]{3,2,1,0:T(8,128)S(1)}, u32[]{:S(2)}, u32[]{:S(2)}) async-start(f32[4,4,32,256]{3,2,1,0:T(8,128)} %cut.1), calls=%async_computation | async-start | bytes 1048576 | tf_op jit(solution)/shard_map/all_to_all | solution.py:479
  8.4 0.0 copy-done.1
  8.4 0.7 copy-done.4
  9.1 0.0 copy-done.6
  9.1 0.0 copy-done.7
  9.1 0.2 pack.1
  9.3 0.0 copy-start.5
  9.3 2.1 %collective-permute-start = (f32[136,256]{1,0:T(8,128)S(1)}, f32[136,256]{1,0:T(8,128)S(1)}, u32[]{:S(2)}, u32[]{:S(2)}) collective-permute-start(f32[136,256]{1,0:T(8,128)S(1)} %get-tuple-element.32), channel_id=1, source_target_pairs={{0,4},{4,0},{8,12},{12,8},{1,5},{5,1},{9,13},{13,9},{2,6},{6,2},{1... | collective-permute-start | bytes 417800 | tf_op jit(solution)/shard_map/ppermute | solution.py:469
  11.4 2.4 %collective-permute-start.1 = (f32[136,256]{1,0:T(8,128)S(1)}, f32[136,256]{1,0:T(8,128)S(1)}, u32[]{:S(2)}, u32[]{:S(2)}) collective-permute-start(f32[136,256]{1,0:T(8,128)S(1)} %get-tuple-element.33), channel_id=1, source_target_pairs={{0,8},{4,12},{8,0},{12,4},{1,9},{5,13},{9,1},{13,5},{2,10},{6,14},... | collective-permute-start | bytes 417800 | tf_op jit(solution)/shard_map/ppermute | solution.py:469
  13.8 0.1 collective-permute-start.2
  13.8 0.0 copy-done.3
  13.8 0.0 copy-done.5
  13.8 0.3 taps.1
  14.1 7.0 %collective-permute-done.refs_1_ = f32[136,256]{1,0:T(8,128)S(1)} collective-permute-done((f32[136,256]{1,0:T(8,128)S(1)}, f32[136,256]{1,0:T(8,128)S(1)}, u32[]{:S(2)}, u32[]{:S(2)}) %collective-permute-start) | collective-permute-done | bytes 139296 | tf_op jit(solution)/shard_map/ppermute | solution.py:469
  21.2 11.7 %collective-permute-done.1.refs_2_ = f32[136,256]{1,0:T(8,128)S(1)} collective-permute-done((f32[136,256]{1,0:T(8,128)S(1)}, f32[136,256]{1,0:T(8,128)S(1)}, u32[]{:S(2)}, u32[]{:S(2)}) %collective-permute-start.1) | collective-permute-done | bytes 139296 | tf_op jit(solution)/shard_map/ppermute | solution.py:469
  32.9 0.0 collective-permute-done.2.refs_3_
  32.9 0.7 copy-done.8
  33.5 2.0 %correct0.1 = (f32[4,72,128]{2,1,0:T(8,128)S(1)}, f32[4,72,128]{2,1,0:T(8,128)S(1)}, f32[4,72,128]{2,1,0:T(8,128)S(1)}, f32[4,72,128]{2,1,0:T(8,128)S(1)}, bf16[...) custom-call(f32[2,12,384]{2,1,0:T(8,128)S(1)} %get-tuple-element.29.line_ref, ...), custom_call_target="tpu_custom_call" | custom-call | tf_op jit(solution)/shard_map/correct0/pallas_call | solution.py:528
  35.5 0.0 all-to-all-done.x_ref
  35.6 2.8 %correct1.1 = f32[16,64,128]{2,1,0:T(8,128)} custom-call(f32[4,4,32,256]{3,2,1,0:T(8,128)S(1)} %all-to-all-done.x_ref, f32[2,12,384]{2,1,0:T(8,128)S(1)} %get-tuple-element.29.line_ref, f32[12,256]{1,0:T(8,128)S(1)} %get-tuple-element.30.gain_ref, bf16[256,256]{1,0:T(8,128)(2,1)S(1)} %get-tuple-element.45.ah_ref, bf16[256,256]{1,0:T(8,128)(2,1)S(1)} %get-tuple-element.46.al_ref), custom_call_target="tpu_custom_call" | custom-call | tf_op jit(solution)/shard_map/correct1/pallas_call | solution.py:551
  38.3 4.9 %all-to-all-start.1 = ((f32[16,64,128]{2,1,0:T(8,128)}), f32[16,64,128]{2,1,0:T(8,128)S(1)}, u32[]{:S(2)}, u32[]{:S(2)}) async-start(f32[16,64,128]{2,1,0:T(8,128)} %correct1.1), calls=%async_computation.1 | async-start | bytes 1048576 | tf_op jit(solution)/shard_map/all_to_all | solution.py:552
  43.2 0.4 collective-permute-start.3
  43.6 1.6 %collective-permute-start.4 = (f32[4,72,128]{2,1,0:T(8,128)S(1)}, f32[4,72,128]{2,1,0:T(8,128)S(1)}, u32[]{:S(2)}, u32[]{:S(2)}) collective-permute-start(f32[4,72,128]{2,1,0:T(8,128)S(1)} %get-tuple-element.37), channel_id=1, source_target_pairs={{0,2},{1,3},{2,0},{3,1},{4,6},{5,7},{6,4},{7,5},{8,10},{9,11},{10,... | collective-permute-start | bytes 442376 | tf_op jit(solution)/shard_map/ppermute | solution.py:419
  45.2 0.0 collective-permute-start.5
  45.2 0.0 collective-permute-done.3.refs_1_
  45.2 9.0 %collective-permute-done.4.refs_2_ = f32[4,72,128]{2,1,0:T(8,128)S(1)} collective-permute-done((f32[4,72,128]{2,1,0:T(8,128)S(1)}, f32[4,72,128]{2,1,0:T(8,128)S(1)}, u32[]{:S(2)}, u32[]{:S(2)}) %collective-permute-start.4) | collective-permute-done | bytes 147488 | tf_op jit(solution)/shard_map/ppermute | solution.py:419
  54.3 3.2 %collective-permute-done.5.refs_3_ = f32[4,72,128]{2,1,0:T(8,128)S(1)} collective-permute-done((f32[4,72,128]{2,1,0:T(8,128)S(1)}, f32[4,72,128]{2,1,0:T(8,128)S(1)}, u32[]{:S(2)}, u32[]{:S(2)}) %collective-permute-start.5) | collective-permute-done | bytes 147488 | tf_op jit(solution)/shard_map/ppermute | solution.py:419
  57.6 1.3 %collective-permute-start.6 = (f32[4,72,128]{2,1,0:T(8,128)S(1)}, f32[4,72,128]{2,1,0:T(8,128)S(1)}, u32[]{:S(2)}, u32[]{:S(2)}) collective-permute-start(f32[4,72,128]{2,1,0:T(8,128)S(1)} %get-tuple-element.40), channel_id=1, source_target_pairs={{0,4},{4,0},{8,12},{12,8},{1,5},{5,1},{9,13},{13,9},{2,6},{6,2},{1... | collective-permute-start | bytes 442376 | tf_op jit(solution)/shard_map/ppermute | solution.py:540
  58.9 2.8 %collective-permute-start.7 = (f32[4,72,128]{2,1,0:T(8,128)S(1)}, f32[4,72,128]{2,1,0:T(8,128)S(1)}, u32[]{:S(2)}, u32[]{:S(2)}) collective-permute-start(f32[4,72,128]{2,1,0:T(8,128)S(1)} %get-tuple-element.41), channel_id=1, source_target_pairs={{0,8},{4,12},{8,0},{12,4},{1,9},{5,13},{9,1},{13,5},{2,10},{6,14},... | collective-permute-start | bytes 442376 | tf_op jit(solution)/shard_map/ppermute | solution.py:540
  61.7 0.3 collective-permute-start.8
  62.0 0.0 copy-done.2
  62.0 4.7 %collective-permute-done.6.refs_1_ = f32[4,72,128]{2,1,0:T(8,128)S(1)} collective-permute-done((f32[4,72,128]{2,1,0:T(8,128)S(1)}, f32[4,72,128]{2,1,0:T(8,128)S(1)}, u32[]{:S(2)}, u32[]{:S(2)}) %collective-permute-start.6) | collective-permute-done | bytes 147488 | tf_op jit(solution)/shard_map/ppermute | solution.py:540
  66.7 6.2 %collective-permute-done.7.refs_2_ = f32[4,72,128]{2,1,0:T(8,128)S(1)} collective-permute-done((f32[4,72,128]{2,1,0:T(8,128)S(1)}, f32[4,72,128]{2,1,0:T(8,128)S(1)}, u32[]{:S(2)}, u32[]{:S(2)}) %collective-permute-start.7) | collective-permute-done | bytes 147488 | tf_op jit(solution)/shard_map/ppermute | solution.py:540
  72.9 0.0 collective-permute-done.8.refs_3_
  72.9 0.4 columns.1
  73.3 0.0 all-to-all-done.1.y_ref
  73.3 1.4 %median.1 = (f32[4,16,128]{2,1,0:T(8,128)S(1)}, f32[4,16,128]{2,1,0:T(8,128)S(1)}) custom-call(f32[16,8,128]{2,1,0:T(8,128)S(1)} %get-tuple-element.43.weight_ref, bf16[128,128]{1,0:T(8,128)(2,1)S(1)} %get-tuple-element.27.kh_ref, bf16[128,128]{1,0:T(8,128)(2,1)S(1)} %get-tuple-element.28.kl_ref, f32[4,4,4,16,128]{4,3,2,1,0:T(8,128)S(1)} %get-tuple-element.44.small_ref, ...), custom_call_target="tpu_custom_call" | custom-call | tf_op jit(solution)/shard_map/median/pallas_call | solution.py:579
  74.7 0.6 collective-permute-start.10
  75.3 0.0 collective-permute-start.11
  75.3 1.6 %collective-permute-start.9 = (f32[4,16,128]{2,1,0:T(8,128)S(1)}, f32[4,16,128]{2,1,0:T(8,128)S(1)}, u32[]{:S(2)}, u32[]{:S(2)}) collective-permute-start(f32[4,16,128]{2,1,0:T(8,128)S(1)} %get-tuple-element.48), channel_id=1, source_target_pairs={{0,1},{1,0},{2,3},{3,2},{4,5},{5,4},{6,7},{7,6},{8,9},{9,8},{10,11... | collective-permute-start | bytes 98312 | tf_op jit(solution)/shard_map/ppermute | solution.py:419
  76.9 2.1 %collective-permute-done.10.refs_2_ = f32[4,16,128]{2,1,0:T(8,128)S(1)} collective-permute-done((f32[4,16,128]{2,1,0:T(8,128)S(1)}, f32[4,16,128]{2,1,0:T(8,128)S(1)}, u32[]{:S(2)}, u32[]{:S(2)}) %collective-permute-start.10) | collective-permute-done | bytes 32800 | tf_op jit(solution)/shard_map/ppermute | solution.py:419
  79.0 0.0 collective-permute-done.11.refs_3_
  79.0 0.0 collective-permute-done.9.refs_1_
  79.0 0.7 place.1
  (8 shorter events, 0.1 us)
Async XLA Ops:
  0.0 1.2 %copy-start = (f32[8,4,32,256]{3,2,1,0:T(8,128)S(1)}, f32[8,4,32,256]{3,2,1,0:T(8,128)}, u32[]{:S(2)}) copy-start(f32[8,4,32,256]{3,2,1,0:T(8,128)} %param.8) | copy-start | bytes 3145732
  1.2 7.2 %copy-start.1 = (f32[8,4,32,256]{3,2,1,0:T(8,128)S(1)}, f32[8,4,32,256]{3,2,1,0:T(8,128)}, u32[]{:S(2)}) copy-start(f32[8,4,32,256]{3,2,1,0:T(8,128)} %param.8) | copy-start | bytes 3145732
  2.1 33.5 %all-to-all-start = ((f32[4,4,32,256]{3,2,1,0:T(8,128)}), f32[4,4,32,256]{3,2,1,0:T(8,128)S(1)}, u32[]{:S(2)}, u32[]{:S(2)}) async-start(f32[4,4,32,256]{3,2,1,0:T(8,128)} %cut.1), calls=%async_computation | async-start | bytes 1048576 | tf_op jit(solution)/shard_map/all_to_all | solution.py:479
  8.4 0.7 copy-start.4
  8.4 0.7 copy-start.6
  8.4 0.7 copy-start.7
  9.1 4.7 %copy-start.3 = (f32[3,4,33]{2,1,0:T(4,128)S(1)}, f32[3,4,33]{2,1,0:T(4,128)}, u32[]{:S(2)}) copy-start(f32[3,4,33]{2,1,0:T(4,128)} %kernels_hbm.1) | copy-start | bytes 4756
  9.3 4.5 %copy-start.5 = (f32[3,4]{1,0:T(4,128)S(1)}, f32[3,4]{1,0:T(4,128)}, u32[]{:S(2)}) copy-start(f32[3,4]{1,0:T(4,128)} %strength_hbm.1) | copy-start | bytes 148
  9.3 11.8 %collective-permute-start = (f32[136,256]{1,0:T(8,128)S(1)}, f32[136,256]{1,0:T(8,128)S(1)}, u32[]{:S(2)}, u32[]{:S(2)}) collective-permute-start(f32[136,256]{1,0:T(8,128)S(1)} %get-tuple-element.32), channel_id=1, source_target_pairs={{0,4},{4,0},{8,12},{12,8},{1,5},{5,1},{9,13},{13,9},{2,6},{6,2},{1... | collective-permute-start | bytes 417800 | tf_op jit(solution)/shard_map/ppermute | solution.py:469
  11.4 21.5 %collective-permute-start.1 = (f32[136,256]{1,0:T(8,128)S(1)}, f32[136,256]{1,0:T(8,128)S(1)}, u32[]{:S(2)}, u32[]{:S(2)}) collective-permute-start(f32[136,256]{1,0:T(8,128)S(1)} %get-tuple-element.33), channel_id=1, source_target_pairs={{0,8},{4,12},{8,0},{12,4},{1,9},{5,13},{9,1},{13,5},{2,10},{6,14},... | collective-permute-start | bytes 417800 | tf_op jit(solution)/shard_map/ppermute | solution.py:469
  13.8 19.1 %collective-permute-start.2 = (f32[136,256]{1,0:T(8,128)S(1)}, f32[136,256]{1,0:T(8,128)S(1)}, u32[]{:S(2)}, u32[]{:S(2)}) collective-permute-start(f32[136,256]{1,0:T(8,128)S(1)} %get-tuple-element.34), channel_id=1, source_target_pairs={{0,12},{4,8},{8,4},{12,0},{1,13},{5,9},{9,5},{13,1},{2,14},{6,10},... | collective-permute-start | bytes 417800 | tf_op jit(solution)/shard_map/ppermute | solution.py:469
  32.9 0.7 copy-start.8
  38.3 34.9 %all-to-all-start.1 = ((f32[16,64,128]{2,1,0:T(8,128)}), f32[16,64,128]{2,1,0:T(8,128)S(1)}, u32[]{:S(2)}, u32[]{:S(2)}) async-start(f32[16,64,128]{2,1,0:T(8,128)} %correct1.1), calls=%async_computation.1 | async-start | bytes 1048576 | tf_op jit(solution)/shard_map/all_to_all | solution.py:552
  43.2 2.0 %collective-permute-start.3 = (f32[4,72,128]{2,1,0:T(8,128)S(1)}, f32[4,72,128]{2,1,0:T(8,128)S(1)}, u32[]{:S(2)}, u32[]{:S(2)}) collective-permute-start(f32[4,72,128]{2,1,0:T(8,128)S(1)} %get-tuple-element.36), channel_id=1, source_target_pairs={{0,1},{1,0},{2,3},{3,2},{4,5},{5,4},{6,7},{7,6},{8,9},{9,8},{10,11... | collective-permute-start | bytes 442376 | tf_op jit(solution)/shard_map/ppermute | solution.py:419
  43.6 10.7 %collective-permute-start.4 = (f32[4,72,128]{2,1,0:T(8,128)S(1)}, f32[4,72,128]{2,1,0:T(8,128)S(1)}, u32[]{:S(2)}, u32[]{:S(2)}) collective-permute-start(f32[4,72,128]{2,1,0:T(8,128)S(1)} %get-tuple-element.37), channel_id=1, source_target_pairs={{0,2},{1,3},{2,0},{3,1},{4,6},{5,7},{6,4},{7,5},{8,10},{9,11},{10,... | collective-permute-start | bytes 442376 | tf_op jit(solution)/shard_map/ppermute | solution.py:419
  45.2 12.3 %collective-permute-start.5 = (f32[4,72,128]{2,1,0:T(8,128)S(1)}, f32[4,72,128]{2,1,0:T(8,128)S(1)}, u32[]{:S(2)}, u32[]{:S(2)}) collective-permute-start(f32[4,72,128]{2,1,0:T(8,128)S(1)} %get-tuple-element.38), channel_id=1, source_target_pairs={{0,3},{1,2},{2,1},{3,0},{4,7},{5,6},{6,5},{7,4},{8,11},{9,10},{10,... | collective-permute-start | bytes 442376 | tf_op jit(solution)/shard_map/ppermute | solution.py:419
  57.5 4.5 %copy-start.2 = (f32[1,128,128]{2,1,0:T(8,128)S(1)}, f32[1,128,128]{2,1,0:T(8,128)}, u32[]{:S(2)}) copy-start(f32[1,128,128]{2,1,0:T(8,128)} %cols_ref.1) | copy-start | bytes 196612
  57.6 9.2 %collective-permute-start.6 = (f32[4,72,128]{2,1,0:T(8,128)S(1)}, f32[4,72,128]{2,1,0:T(8,128)S(1)}, u32[]{:S(2)}, u32[]{:S(2)}) collective-permute-start(f32[4,72,128]{2,1,0:T(8,128)S(1)} %get-tuple-element.40), channel_id=1, source_target_pairs={{0,4},{4,0},{8,12},{12,8},{1,5},{5,1},{9,13},{13,9},{2,6},{6,2},{1... | collective-permute-start | bytes 442376 | tf_op jit(solution)/shard_map/ppermute | solution.py:540
  58.9 14.0 %collective-permute-start.7 = (f32[4,72,128]{2,1,0:T(8,128)S(1)}, f32[4,72,128]{2,1,0:T(8,128)S(1)}, u32[]{:S(2)}, u32[]{:S(2)}) collective-permute-start(f32[4,72,128]{2,1,0:T(8,128)S(1)} %get-tuple-element.41), channel_id=1, source_target_pairs={{0,8},{4,12},{8,0},{12,4},{1,9},{5,13},{9,1},{13,5},{2,10},{6,14},... | collective-permute-start | bytes 442376 | tf_op jit(solution)/shard_map/ppermute | solution.py:540
  61.7 11.1 %collective-permute-start.8 = (f32[4,72,128]{2,1,0:T(8,128)S(1)}, f32[4,72,128]{2,1,0:T(8,128)S(1)}, u32[]{:S(2)}, u32[]{:S(2)}) collective-permute-start(f32[4,72,128]{2,1,0:T(8,128)S(1)} %get-tuple-element.42), channel_id=1, source_target_pairs={{0,12},{4,8},{8,4},{12,0},{1,13},{5,9},{9,5},{13,1},{2,14},{6,10},... | collective-permute-start | bytes 442376 | tf_op jit(solution)/shard_map/ppermute | solution.py:540
  74.7 4.3 %collective-permute-start.10 = (f32[4,16,128]{2,1,0:T(8,128)S(1)}, f32[4,16,128]{2,1,0:T(8,128)S(1)}, u32[]{:S(2)}, u32[]{:S(2)}) collective-permute-start(f32[4,16,128]{2,1,0:T(8,128)S(1)} %get-tuple-element.47.refs_0_), channel_id=1, source_target_pairs={{0,2},{1,3},{2,0},{3,1},{4,6},{5,7},{6,4},{7,5},{8,10},{9,11},{10,... | collective-permute-start | bytes 98312 | tf_op jit(solution)/shard_map/ppermute | solution.py:419
  75.3 3.7 %collective-permute-start.11 = (f32[4,16,128]{2,1,0:T(8,128)S(1)}, f32[4,16,128]{2,1,0:T(8,128)S(1)}, u32[]{:S(2)}, u32[]{:S(2)}) collective-permute-start(f32[4,16,128]{2,1,0:T(8,128)S(1)} %get-tuple-element.48), channel_id=1, source_target_pairs={{0,3},{1,2},{2,1},{3,0},{4,7},{5,6},{6,5},{7,4},{8,11},{9,10},{10,... | collective-permute-start | bytes 98312 | tf_op jit(solution)/shard_map/ppermute | solution.py:419
  75.3 3.7 %collective-permute-start.9 = (f32[4,16,128]{2,1,0:T(8,128)S(1)}, f32[4,16,128]{2,1,0:T(8,128)S(1)}, u32[]{:S(2)}, u32[]{:S(2)}) collective-permute-start(f32[4,16,128]{2,1,0:T(8,128)S(1)} %get-tuple-element.48), channel_id=1, source_target_pairs={{0,1},{1,0},{2,3},{3,2},{4,5},{5,4},{6,7},{7,6},{8,9},{9,8},{10,11... | collective-permute-start | bytes 98312 | tf_op jit(solution)/shard_map/ppermute | solution.py:419

commit v3 on v2

--- a/solution.py
+++ b/solution.py
@@ -72,6 +72,7 @@
     target_hbm,
     start_hbm,
     rows_hbm,
+    count_hbm,
     images_ref,
     *refs,
     part,
@@ -79,11 +80,11 @@
     table_lines,
 ):
     spaces, _, strip, width = images_ref.shape
-    outs, (target_ref, start_ref, rows_ref, sem) = refs[:spaces], refs[spaces:]
+    outs, (target_ref, start_ref, rows_ref, count_ref, sem) = refs[:spaces], refs[spaces:]
     tables = fetch(
         zip(
-            (target_hbm, start_hbm, rows_hbm),
-            (target_ref, start_ref, rows_ref),
+            (target_hbm, start_hbm, rows_hbm, count_hbm),
+            (target_ref, start_ref, rows_ref, count_ref),
         ),
         sem,
     )
@@ -120,6 +121,8 @@
                 at = size + BROWS + t * table_lines + k
                 used = min(width, length - k * width)
                 out[at : at + 1, 0:used] = line[:, k * width : k * width + used]
+        at = size + BROWS + 2 * table_lines
+        out[at : at + 1, 0 : count_ref.shape[1]] = count_ref[...].astype(f32)
 
 
 def cut_kernel(images_ref, out_ref):
@@ -207,7 +210,7 @@
 
 
 def small_kernel(
-    line_ref, gain_ref, count_ref, *refs, spaces, cores, passes, bands, radius, share, table_lines
+    line_ref, gain_ref, *refs, spaces, cores, passes, bands, radius, share, table_lines
 ):
     x_refs, (*out_refs, ah_ref, al_ref, state, laid_ref) = refs[:spaces], refs[spaces:]
     part, rows, width = state.shape
@@ -256,11 +259,11 @@
                     out[g, j * share : (j + 1) * share, :] = lines[
                         :, p * BCOLS : (p + 1) * BCOLS
                     ]
-    counts = count_ref[...].astype(f32)
+    at = tables + BROWS + 2 * table_lines
+    counted = [ref[at : at + 1, 0:BCOLS] for ref in x_refs]
     for out in out_refs:
-        for g in range(spaces):
-            out[g, part * share :, :] = jnp.zeros((SUBLANES, BCOLS), f32)
-            out[g, part * share : part * share + 1, 0 : counts.shape[1]] = counts
+        out[0, part * share : part * share + 1, :] = counted[0]
+        out[0, part * share + 1 : part * share + 2, :] = total(counted)
 
 
 def large_kernel(
@@ -291,28 +294,29 @@
 
 
 def regroup_kernel(*refs, spaces):
-    groups = len(refs) - spaces
+    groups, size = refs[-2].shape[:2]
     own = lax.axis_index("space")
-    for d in range(spaces):
-        for k in range(groups):
-            refs[groups + d][k] = refs[k][own ^ d]
+    for k in range(groups):
+        for d in range(spaces):
+            refs[groups + d][k] = refs[k][own ^ d, :size, :]
+        refs[-1][k] = refs[k][0, size:, :]
 
 
 def columns_kernel(
-    kh_ref, kl_ref, *refs, spaces, dates, cores, local_dates
+    kh_ref, kl_ref, count_ref, *refs, spaces, dates, cores, local_dates
 ):
     y_refs, (full_ref, weight_ref) = refs[:spaces], refs[spaces:]
     sides, part, share, width = full_ref.shape[1:]
     size = part * share
     kh, kl = kh_ref[...], kl_ref[...]
     for d in range(spaces):
-        block = y_refs[d][:, :size, :].reshape(sides * size, width)
+        block = y_refs[d][...].reshape(sides * size, width)
         full_ref[d] = columns_of(block, kh, kl).reshape(sides, part, share, width)
-    counted = [y[dx * cores, size : size + 1, :] for y in y_refs for dx in range(dates)]
-    summed = jnp.sum(total(counted), axis=1, keepdims=True)
+    counted = total(count_ref[dx * cores, 1:2, :] for dx in range(dates))
+    summed = jnp.sum(counted, axis=1, keepdims=True)
     mean_count = summed / f32(spaces * dates * local_dates)
     for dx in range(dates):
-        own = y_refs[0][dx * cores, size : size + 1, :]
+        own = count_ref[dx * cores, 0:1, :]
         weight = own / (own + mean_count)
         for t in range(local_dates):
             weight_ref[dx * local_dates + t] = jnp.broadcast_to(
@@ -442,17 +446,18 @@
         functools.partial(pack_kernel, part=part, halves=halves, table_lines=table_lines),
         out_shape=[
             jax.ShapeDtypeStruct(
-                (part * strip + round_up(BROWS + 2 * table_lines, SUBLANES), width), f32
+                (part * strip + round_up(BROWS + 2 * table_lines + 1, SUBLANES), width), f32
             )
         ]
         * spaces,
-        in_specs=hbm(3) + vmem(1),
+        in_specs=hbm(4) + vmem(1),
         out_specs=vmem(spaces),
         scratch_shapes=[
             pltpu.VMEM((1, blocks), jnp.int32),
             pltpu.VMEM((1, blocks), jnp.int32),
             pltpu.VMEM((1, BROWS, BROWS), f32),
-            pltpu.SemaphoreType.DMA((3,)),
+            pltpu.VMEM((1, local_dates), jnp.int32),
+            pltpu.SemaphoreType.DMA((4,)),
         ],
         compiler_params=params(4),
         name="pack",
@@ -462,6 +467,7 @@
             destinations.reshape(1, blocks),
             offsets.reshape(1, blocks),
             resample_rows,
+            counts.reshape(1, local_dates),
             images,
         )
     )
@@ -516,7 +522,7 @@
         ),
         out_shape=[jax.ShapeDtypeStruct((spaces, small_rows, BCOLS), f32)] * (dates * cores)
         + [jax.ShapeDtypeStruct((spaces * tile_rows, length), bf16)] * 2,
-        in_specs=vmem(3 + spaces),
+        in_specs=vmem(2 + spaces),
         out_specs=vmem(dates * cores + 2),
         scratch_shapes=[
             pltpu.VMEM((part, rows, width), f32),
@@ -525,17 +531,18 @@
         compiler_params=params(20),
         name="correct0",
     )
-    *sides, ah, al = correct_small(lines, gains, counts.reshape(1, local_dates), *small)
+    *sides, ah, al = correct_small(lines, gains, *small)
     sides = across_sides(sides, dates, cores)
     regroup = pl.pallas_call(
         functools.partial(regroup_kernel, spaces=spaces),
-        out_shape=[jax.ShapeDtypeStruct((dates * cores, small_rows, BCOLS), f32)] * spaces,
+        out_shape=[jax.ShapeDtypeStruct((dates * cores, part * share, BCOLS), f32)] * spaces
+        + [jax.ShapeDtypeStruct((dates * cores, SUBLANES, BCOLS), f32)],
         in_specs=vmem(dates * cores),
-        out_specs=vmem(spaces),
+        out_specs=vmem(spaces + 1),
         compiler_params=params(4),
         name="regroup",
     )
-    small = list(regroup(*sides))
+    *small, counted = regroup(*sides)
     for d in range(spaces - 1, 0, -1):
         small[d] = lax.ppermute(small[d], "space", [(i, i ^ d) for i in range(spaces)])
 
@@ -570,12 +577,12 @@
             jax.ShapeDtypeStruct((spaces, dates * cores, part, share, BCOLS), f32),
             jax.ShapeDtypeStruct((dates * local_dates, tile, BCOLS), f32),
         ],
-        in_specs=vmem(2 + spaces),
+        in_specs=vmem(3 + spaces),
         out_specs=vmem(2),
         compiler_params=params(8),
         name="columns",
     )
-    full, weights = columns_call(*columns, *small)
+    full, weights = columns_call(*columns, counted, *small)
     shares = pl.pallas_call(
         functools.partial(
             median_kernel,

time: 80.4 us -> 78.4 us (0.975)
  waiting for transfers between devices: 43.9 us -> 42.9 us
    ppermute x6, waiting for transfers between devices: 29.6 us -> 28.5 us  [local(): lax.ppermute(small[d], 'space', [(i, i ^ d) for i in range(spaces)])]
where the time goes in v3:
time: 78.4 us; the launch traced here: 77.9 us
  waiting for transfers between devices  42.9 us (55%)
  starting transfers between devices  24.4 us (31%)
  Pallas kernels  8.61 us (11%)
  local copies, waits for them, and re-layouts  1.92 us (2%)
    ppermute x6, waiting for transfers between devices, local(): lax.ppermute(small[d], 'space', [(i, i ^ d) for i in range(spaces)])  28.5 us
    ppermute x6, waiting for transfers between devices, across_sides(): received.append(lax.ppermute(pieces[k], ('date', 'band'), pairs))  14.4 us
    ppermute x6, starting transfers between devices, local(): lax.ppermute(small[d], 'space', [(i, i ^ d) for i in range(spaces)])  8.98 us
    all_to_all x1, starting transfers between devices, local(): lax.all_to_all(rest, 'space', split_axis=0, concat_axis=0, tiled=True)  6.35 us
    all_to_all x1, starting transfers between devices, local(): lax.all_to_all(laid, ('space', 'date', 'band'), split_axis=0, concat_axis...  4.85 us
    ppermute x6, starting transfers between devices, across_sides(): received.append(lax.ppermute(pieces[k], ('date', 'band'), pairs))  4.25 us
    pallas_call x1, Pallas kernels, local(): laid = correct_large(large, lines, gains, ah, al)  2.77 us
    pallas_call x1, Pallas kernels, local(): *sides, ah, al = correct_small(lines, gains, *small)  2.03 us
  transfers between devices with their start and end apart: 14, of which 7 were waited for; matrix products, arithmetic and copies ran while one was open for 0% of the time, Pallas kernels for 4%

profile of v3, /device:TPU:0, one launch (start us, length us, event | category | flops | bytes accessed | tf_op | source)
XLA Modules:
  0.0 77.9 jit_solution(17733887634790769529)
XLA Ops:
  0.0 0.0 copy-start
  0.0 1.2 %copy-done = f32[8,4,32,256]{3,2,1,0:T(8,128)S(1)} copy-done((f32[8,4,32,256]{3,2,1,0:T(8,128)S(1)}, f32[8,4,32,256]{3,2,1,0:T(8,128)}, u32[]{:S(2)}) %copy-start) | copy-done | bytes 1048600
  1.2 0.8 %cut.1 = f32[4,4,32,256]{3,2,1,0:T(8,128)} custom-call(f32[4,8,32,256]{3,2,1,0:T(8,128)S(1)} %bitcast.4), custom_call_target="tpu_custom_call" | custom-call | tf_op jit(solution)/shard_map/cut/pallas_call | solution.py:484
  2.1 6.3 %all-to-all-start = ((f32[4,4,32,256]{3,2,1,0:T(8,128)}), f32[4,4,32,256]{3,2,1,0:T(8,128)S(1)}, u32[]{:S(2)}, u32[]{:S(2)}) async-start(f32[4,4,32,256]{3,2,1,0:T(8,128)} %cut.1), calls=%async_computation | async-start | bytes 1048576 | tf_op jit(solution)/shard_map/all_to_all | solution.py:485
  8.4 0.0 copy-start.8
  8.4 0.0 copy-done.1
  8.5 0.7 copy-done.4
  9.1 0.0 copy-done.6
  9.1 0.0 copy-done.7
  9.1 0.0 copy-done.8
  9.1 0.2 pack.1
  9.3 0.0 copy-start.5
  9.3 2.1 %collective-permute-start = (f32[136,256]{1,0:T(8,128)S(1)}, f32[136,256]{1,0:T(8,128)S(1)}, u32[]{:S(2)}, u32[]{:S(2)}) collective-permute-start(f32[136,256]{1,0:T(8,128)S(1)} %get-tuple-element.33), channel_id=1, source_target_pairs={{0,4},{4,0},{8,12},{12,8},{1,5},{5,1},{9,13},{13,9},{2,6},{6,2},{1... | collective-permute-start | bytes 417800 | tf_op jit(solution)/shard_map/ppermute | solution.py:475
  11.4 2.4 %collective-permute-start.1 = (f32[136,256]{1,0:T(8,128)S(1)}, f32[136,256]{1,0:T(8,128)S(1)}, u32[]{:S(2)}, u32[]{:S(2)}) collective-permute-start(f32[136,256]{1,0:T(8,128)S(1)} %get-tuple-element.34), channel_id=1, source_target_pairs={{0,8},{4,12},{8,0},{12,4},{1,9},{5,13},{9,1},{13,5},{2,10},{6,14},... | collective-permute-start | bytes 417800 | tf_op jit(solution)/shard_map/ppermute | solution.py:475
  13.8 0.1 collective-permute-start.2
  13.9 0.0 copy-done.3
  13.9 0.0 copy-done.5
  13.9 0.3 taps.1
  14.2 7.0 %collective-permute-done.refs_1_ = f32[136,256]{1,0:T(8,128)S(1)} collective-permute-done((f32[136,256]{1,0:T(8,128)S(1)}, f32[136,256]{1,0:T(8,128)S(1)}, u32[]{:S(2)}, u32[]{:S(2)}) %collective-permute-start) | collective-permute-done | bytes 139296 | tf_op jit(solution)/shard_map/ppermute | solution.py:475
  21.2 11.7 %collective-permute-done.1.refs_2_ = f32[136,256]{1,0:T(8,128)S(1)} collective-permute-done((f32[136,256]{1,0:T(8,128)S(1)}, f32[136,256]{1,0:T(8,128)S(1)}, u32[]{:S(2)}, u32[]{:S(2)}) %collective-permute-start.1) | collective-permute-done | bytes 139296 | tf_op jit(solution)/shard_map/ppermute | solution.py:475
  32.9 0.0 collective-permute-done.2.refs_3_
  32.9 2.0 %correct0.1 = (f32[4,72,128]{2,1,0:T(8,128)S(1)}, f32[4,72,128]{2,1,0:T(8,128)S(1)}, f32[4,72,128]{2,1,0:T(8,128)S(1)}, f32[4,72,128]{2,1,0:T(8,128)S(1)}, bf16[...) custom-call(f32[2,12,384]{2,1,0:T(8,128)S(1)} %get-tuple-element.30.line_ref, ...), custom_call_target="tpu_custom_call" | custom-call | tf_op jit(solution)/shard_map/correct0/pallas_call | solution.py:534
  34.9 0.0 all-to-all-done.x_ref
  34.9 2.8 %correct1.1 = f32[16,64,128]{2,1,0:T(8,128)} custom-call(f32[4,4,32,256]{3,2,1,0:T(8,128)S(1)} %all-to-all-done.x_ref, f32[2,12,384]{2,1,0:T(8,128)S(1)} %get-tuple-element.30.line_ref, f32[12,256]{1,0:T(8,128)S(1)} %get-tuple-element.31.gain_ref, bf16[256,256]{1,0:T(8,128)(2,1)S(1)} %get-tuple-element.47.ah_ref, bf16[256,256]{1,0:T(8,128)(2,1)S(1)} %get-tuple-element.48.al_ref), custom_call_target="tpu_custom_call" | custom-call | tf_op jit(solution)/shard_map/correct1/pallas_call | solution.py:558
  37.7 4.9 %all-to-all-start.1 = ((f32[16,64,128]{2,1,0:T(8,128)}), f32[16,64,128]{2,1,0:T(8,128)S(1)}, u32[]{:S(2)}, u32[]{:S(2)}) async-start(f32[16,64,128]{2,1,0:T(8,128)} %correct1.1), calls=%async_computation.1 | async-start | bytes 1048576 | tf_op jit(solution)/shard_map/all_to_all | solution.py:559
  42.5 0.4 collective-permute-start.3
  42.9 1.6 %collective-permute-start.4 = (f32[4,72,128]{2,1,0:T(8,128)S(1)}, f32[4,72,128]{2,1,0:T(8,128)S(1)}, u32[]{:S(2)}, u32[]{:S(2)}) collective-permute-start(f32[4,72,128]{2,1,0:T(8,128)S(1)} %get-tuple-element.38), channel_id=1, source_target_pairs={{0,2},{1,3},{2,0},{3,1},{4,6},{5,7},{6,4},{7,5},{8,10},{9,11},{10,... | collective-permute-start | bytes 442376 | tf_op jit(solution)/shard_map/ppermute | solution.py:423
  44.6 0.0 collective-permute-start.5
  44.6 0.0 collective-permute-done.3.refs_1_
  44.6 9.0 %collective-permute-done.4.refs_2_ = f32[4,72,128]{2,1,0:T(8,128)S(1)} collective-permute-done((f32[4,72,128]{2,1,0:T(8,128)S(1)}, f32[4,72,128]{2,1,0:T(8,128)S(1)}, u32[]{:S(2)}, u32[]{:S(2)}) %collective-permute-start.4) | collective-permute-done | bytes 147488 | tf_op jit(solution)/shard_map/ppermute | solution.py:423
  53.6 3.2 %collective-permute-done.5.refs_3_ = f32[4,72,128]{2,1,0:T(8,128)S(1)} collective-permute-done((f32[4,72,128]{2,1,0:T(8,128)S(1)}, f32[4,72,128]{2,1,0:T(8,128)S(1)}, u32[]{:S(2)}, u32[]{:S(2)}) %collective-permute-start.5) | collective-permute-done | bytes 147488 | tf_op jit(solution)/shard_map/ppermute | solution.py:423
  56.9 1.3 %collective-permute-start.6 = (f32[4,64,128]{2,1,0:T(8,128)S(1)}, f32[4,64,128]{2,1,0:T(8,128)S(1)}, u32[]{:S(2)}, u32[]{:S(2)}) collective-permute-start(f32[4,64,128]{2,1,0:T(8,128)S(1)} %get-tuple-element.42), channel_id=1, source_target_pairs={{0,4},{4,0},{8,12},{12,8},{1,5},{5,1},{9,13},{13,9},{2,6},{6,2},{1... | collective-permute-start | bytes 393224 | tf_op jit(solution)/shard_map/ppermute | solution.py:547
  58.2 2.8 %collective-permute-start.7 = (f32[4,64,128]{2,1,0:T(8,128)S(1)}, f32[4,64,128]{2,1,0:T(8,128)S(1)}, u32[]{:S(2)}, u32[]{:S(2)}) collective-permute-start(f32[4,64,128]{2,1,0:T(8,128)S(1)} %get-tuple-element.43), channel_id=1, source_target_pairs={{0,8},{4,12},{8,0},{12,4},{1,9},{5,13},{9,1},{13,5},{2,10},{6,14},... | collective-permute-start | bytes 393224 | tf_op jit(solution)/shard_map/ppermute | solution.py:547
  61.1 0.3 collective-permute-start.8
  61.3 0.0 copy-done.2
  61.4 3.9 %collective-permute-done.6.refs_1_ = f32[4,64,128]{2,1,0:T(8,128)S(1)} collective-permute-done((f32[4,64,128]{2,1,0:T(8,128)S(1)}, f32[4,64,128]{2,1,0:T(8,128)S(1)}, u32[]{:S(2)}, u32[]{:S(2)}) %collective-permute-start.6) | collective-permute-done | bytes 131104 | tf_op jit(solution)/shard_map/ppermute | solution.py:547
  65.3 5.9 %collective-permute-done.7.refs_2_ = f32[4,64,128]{2,1,0:T(8,128)S(1)} collective-permute-done((f32[4,64,128]{2,1,0:T(8,128)S(1)}, f32[4,64,128]{2,1,0:T(8,128)S(1)}, u32[]{:S(2)}, u32[]{:S(2)}) %collective-permute-start.7) | collective-permute-done | bytes 131104 | tf_op jit(solution)/shard_map/ppermute | solution.py:547
  71.2 0.0 collective-permute-done.8.refs_3_
  71.2 0.4 columns.1
  71.5 0.0 all-to-all-done.1.y_ref
  71.5 1.4 %median.1 = (f32[4,16,128]{2,1,0:T(8,128)S(1)}, f32[4,16,128]{2,1,0:T(8,128)S(1)}) custom-call(f32[16,8,128]{2,1,0:T(8,128)S(1)} %get-tuple-element.45.weight_ref, bf16[128,128]{1,0:T(8,128)(2,1)S(1)} %get-tuple-element.28.kh_ref, bf16[128,128]{1,0:T(8,128)(2,1)S(1)} %get-tuple-element.29.kl_ref, f32[4,4,4,16,128]{4,3,2,1,0:T(8,128)S(1)} %get-tuple-element.46.small_ref, ...), custom_call_target="tpu_custom_call" | custom-call | tf_op jit(solution)/shard_map/median/pallas_call | solution.py:586
  72.9 0.6 collective-permute-start.10
  73.6 0.0 collective-permute-start.11
  73.6 1.6 %collective-permute-start.9 = (f32[4,16,128]{2,1,0:T(8,128)S(1)}, f32[4,16,128]{2,1,0:T(8,128)S(1)}, u32[]{:S(2)}, u32[]{:S(2)}) collective-permute-start(f32[4,16,128]{2,1,0:T(8,128)S(1)} %get-tuple-element.50), channel_id=1, source_target_pairs={{0,1},{1,0},{2,3},{3,2},{4,5},{5,4},{6,7},{7,6},{8,9},{9,8},{10,11... | collective-permute-start | bytes 98312 | tf_op jit(solution)/shard_map/ppermute | solution.py:423
  75.2 2.1 %collective-permute-done.10.refs_2_ = f32[4,16,128]{2,1,0:T(8,128)S(1)} collective-permute-done((f32[4,16,128]{2,1,0:T(8,128)S(1)}, f32[4,16,128]{2,1,0:T(8,128)S(1)}, u32[]{:S(2)}, u32[]{:S(2)}) %collective-permute-start.10) | collective-permute-done | bytes 32800 | tf_op jit(solution)/shard_map/ppermute | solution.py:423
  77.3 0.0 collective-permute-done.11.refs_3_
  77.3 0.0 collective-permute-done.9.refs_1_
  77.3 0.7 place.1
  (8 shorter events, 0.1 us)
Async XLA Ops:
  0.0 1.2 %copy-start = (f32[8,4,32,256]{3,2,1,0:T(8,128)S(1)}, f32[8,4,32,256]{3,2,1,0:T(8,128)}, u32[]{:S(2)}) copy-start(f32[8,4,32,256]{3,2,1,0:T(8,128)} %param.8) | copy-start | bytes 3145732
  1.2 7.2 %copy-start.1 = (f32[8,4,32,256]{3,2,1,0:T(8,128)S(1)}, f32[8,4,32,256]{3,2,1,0:T(8,128)}, u32[]{:S(2)}) copy-start(f32[8,4,32,256]{3,2,1,0:T(8,128)} %param.8) | copy-start | bytes 3145732
  2.1 32.8 %all-to-all-start = ((f32[4,4,32,256]{3,2,1,0:T(8,128)}), f32[4,4,32,256]{3,2,1,0:T(8,128)S(1)}, u32[]{:S(2)}, u32[]{:S(2)}) async-start(f32[4,4,32,256]{3,2,1,0:T(8,128)} %cut.1), calls=%async_computation | async-start | bytes 1048576 | tf_op jit(solution)/shard_map/all_to_all | solution.py:485
  8.4 0.7 copy-start.4
  8.4 0.7 copy-start.6
  8.4 0.7 copy-start.7
  8.4 0.7 copy-start.8
  9.1 4.8 %copy-start.3 = (f32[3,4,33]{2,1,0:T(4,128)S(1)}, f32[3,4,33]{2,1,0:T(4,128)}, u32[]{:S(2)}) copy-start(f32[3,4,33]{2,1,0:T(4,128)} %kernels_hbm.1) | copy-start | bytes 4756
  9.3 4.5 %copy-start.5 = (f32[3,4]{1,0:T(4,128)S(1)}, f32[3,4]{1,0:T(4,128)}, u32[]{:S(2)}) copy-start(f32[3,4]{1,0:T(4,128)} %strength_hbm.1) | copy-start | bytes 148
  9.3 11.8 %collective-permute-start = (f32[136,256]{1,0:T(8,128)S(1)}, f32[136,256]{1,0:T(8,128)S(1)}, u32[]{:S(2)}, u32[]{:S(2)}) collective-permute-start(f32[136,256]{1,0:T(8,128)S(1)} %get-tuple-element.33), channel_id=1, source_target_pairs={{0,4},{4,0},{8,12},{12,8},{1,5},{5,1},{9,13},{13,9},{2,6},{6,2},{1... | collective-permute-start | bytes 417800 | tf_op jit(solution)/shard_map/ppermute | solution.py:475
  11.4 21.4 %collective-permute-start.1 = (f32[136,256]{1,0:T(8,128)S(1)}, f32[136,256]{1,0:T(8,128)S(1)}, u32[]{:S(2)}, u32[]{:S(2)}) collective-permute-start(f32[136,256]{1,0:T(8,128)S(1)} %get-tuple-element.34), channel_id=1, source_target_pairs={{0,8},{4,12},{8,0},{12,4},{1,9},{5,13},{9,1},{13,5},{2,10},{6,14},... | collective-permute-start | bytes 417800 | tf_op jit(solution)/shard_map/ppermute | solution.py:475
  13.8 19.1 %collective-permute-start.2 = (f32[136,256]{1,0:T(8,128)S(1)}, f32[136,256]{1,0:T(8,128)S(1)}, u32[]{:S(2)}, u32[]{:S(2)}) collective-permute-start(f32[136,256]{1,0:T(8,128)S(1)} %get-tuple-element.35), channel_id=1, source_target_pairs={{0,12},{4,8},{8,4},{12,0},{1,13},{5,9},{9,5},{13,1},{2,14},{6,10},... | collective-permute-start | bytes 417800 | tf_op jit(solution)/shard_map/ppermute | solution.py:475
  37.7 33.8 %all-to-all-start.1 = ((f32[16,64,128]{2,1,0:T(8,128)}), f32[16,64,128]{2,1,0:T(8,128)S(1)}, u32[]{:S(2)}, u32[]{:S(2)}) async-start(f32[16,64,128]{2,1,0:T(8,128)} %correct1.1), calls=%async_computation.1 | async-start | bytes 1048576 | tf_op jit(solution)/shard_map/all_to_all | solution.py:559
  42.5 2.0 %collective-permute-start.3 = (f32[4,72,128]{2,1,0:T(8,128)S(1)}, f32[4,72,128]{2,1,0:T(8,128)S(1)}, u32[]{:S(2)}, u32[]{:S(2)}) collective-permute-start(f32[4,72,128]{2,1,0:T(8,128)S(1)} %get-tuple-element.37), channel_id=1, source_target_pairs={{0,1},{1,0},{2,3},{3,2},{4,5},{5,4},{6,7},{7,6},{8,9},{9,8},{10,11... | collective-permute-start | bytes 442376 | tf_op jit(solution)/shard_map/ppermute | solution.py:423
  42.9 10.7 %collective-permute-start.4 = (f32[4,72,128]{2,1,0:T(8,128)S(1)}, f32[4,72,128]{2,1,0:T(8,128)S(1)}, u32[]{:S(2)}, u32[]{:S(2)}) collective-permute-start(f32[4,72,128]{2,1,0:T(8,128)S(1)} %get-tuple-element.38), channel_id=1, source_target_pairs={{0,2},{1,3},{2,0},{3,1},{4,6},{5,7},{6,4},{7,5},{8,10},{9,11},{10,... | collective-permute-start | bytes 442376 | tf_op jit(solution)/shard_map/ppermute | solution.py:423
  44.6 12.3 %collective-permute-start.5 = (f32[4,72,128]{2,1,0:T(8,128)S(1)}, f32[4,72,128]{2,1,0:T(8,128)S(1)}, u32[]{:S(2)}, u32[]{:S(2)}) collective-permute-start(f32[4,72,128]{2,1,0:T(8,128)S(1)} %get-tuple-element.39), channel_id=1, source_target_pairs={{0,3},{1,2},{2,1},{3,0},{4,7},{5,6},{6,5},{7,4},{8,11},{9,10},{10,... | collective-permute-start | bytes 442376 | tf_op jit(solution)/shard_map/ppermute | solution.py:423
  56.8 4.5 %copy-start.2 = (f32[1,128,128]{2,1,0:T(8,128)S(1)}, f32[1,128,128]{2,1,0:T(8,128)}, u32[]{:S(2)}) copy-start(f32[1,128,128]{2,1,0:T(8,128)} %cols_ref.1) | copy-start | bytes 196612
  56.9 8.4 %collective-permute-start.6 = (f32[4,64,128]{2,1,0:T(8,128)S(1)}, f32[4,64,128]{2,1,0:T(8,128)S(1)}, u32[]{:S(2)}, u32[]{:S(2)}) collective-permute-start(f32[4,64,128]{2,1,0:T(8,128)S(1)} %get-tuple-element.42), channel_id=1, source_target_pairs={{0,4},{4,0},{8,12},{12,8},{1,5},{5,1},{9,13},{13,9},{2,6},{6,2},{1... | collective-permute-start | bytes 393224 | tf_op jit(solution)/shard_map/ppermute | solution.py:547
  58.2 12.9 %collective-permute-start.7 = (f32[4,64,128]{2,1,0:T(8,128)S(1)}, f32[4,64,128]{2,1,0:T(8,128)S(1)}, u32[]{:S(2)}, u32[]{:S(2)}) collective-permute-start(f32[4,64,128]{2,1,0:T(8,128)S(1)} %get-tuple-element.43), channel_id=1, source_target_pairs={{0,8},{4,12},{8,0},{12,4},{1,9},{5,13},{9,1},{13,5},{2,10},{6,14},... | collective-permute-start | bytes 393224 | tf_op jit(solution)/shard_map/ppermute | solution.py:547
  61.1 10.1 %collective-permute-start.8 = (f32[4,64,128]{2,1,0:T(8,128)S(1)}, f32[4,64,128]{2,1,0:T(8,128)S(1)}, u32[]{:S(2)}, u32[]{:S(2)}) collective-permute-start(f32[4,64,128]{2,1,0:T(8,128)S(1)} %get-tuple-element.44), channel_id=1, source_target_pairs={{0,12},{4,8},{8,4},{12,0},{1,13},{5,9},{9,5},{13,1},{2,14},{6,10},... | collective-permute-start | bytes 393224 | tf_op jit(solution)/shard_map/ppermute | solution.py:547
  72.9 4.3 %collective-permute-start.10 = (f32[4,16,128]{2,1,0:T(8,128)S(1)}, f32[4,16,128]{2,1,0:T(8,128)S(1)}, u32[]{:S(2)}, u32[]{:S(2)}) collective-permute-start(f32[4,16,128]{2,1,0:T(8,128)S(1)} %get-tuple-element.49.refs_0_), channel_id=1, source_target_pairs={{0,2},{1,3},{2,0},{3,1},{4,6},{5,7},{6,4},{7,5},{8,10},{9,11},{10,... | collective-permute-start | bytes 98312 | tf_op jit(solution)/shard_map/ppermute | solution.py:423
  73.6 3.7 %collective-permute-start.11 = (f32[4,16,128]{2,1,0:T(8,128)S(1)}, f32[4,16,128]{2,1,0:T(8,128)S(1)}, u32[]{:S(2)}, u32[]{:S(2)}) collective-permute-start(f32[4,16,128]{2,1,0:T(8,128)S(1)} %get-tuple-element.50), channel_id=1, source_target_pairs={{0,3},{1,2},{2,1},{3,0},{4,7},{5,6},{6,5},{7,4},{8,11},{9,10},{10,... | collective-permute-start | bytes 98312 | tf_op jit(solution)/shard_map/ppermute | solution.py:423
  73.6 3.7 %collective-permute-start.9 = (f32[4,16,128]{2,1,0:T(8,128)S(1)}, f32[4,16,128]{2,1,0:T(8,128)S(1)}, u32[]{:S(2)}, u32[]{:S(2)}) collective-permute-start(f32[4,16,128]{2,1,0:T(8,128)S(1)} %get-tuple-element.50), channel_id=1, source_target_pairs={{0,1},{1,0},{2,3},{3,2},{4,5},{5,4},{6,7},{7,6},{8,9},{9,8},{10,11... | collective-permute-start | bytes 98312 | tf_op jit(solution)/shard_map/ppermute | solution.py:423

commit v4 on v3

--- a/solution.py
+++ b/solution.py
@@ -267,19 +267,27 @@
 
 
 def large_kernel(
-    x_ref, line_ref, gain_ref, ah_ref, al_ref, out_ref, state, *, first, passes, bands, radius
+    x_ref, line_ref, gain_ref, ah_ref, al_ref, out_ref, state, piece, sem, *, first, passes, bands, radius
 ):
     spaces, part = x_ref.shape[:2]
     for i in range(part):
         state[i] = jnp.concatenate([x_ref[s, i] for s in range(spaces)], axis=0)
     corrections(state, line_ref, gain_ref, first, passes, bands, radius)
     share = out_ref.shape[1] // part
+    copies = []
     for pair, laid in laid_pairs(state, ah_ref[...], al_ref[...]):
         for p, j in enumerate(pair):
             for d in range(out_ref.shape[0]):
-                out_ref[d, j * share : (j + 1) * share, :] = laid[
+                piece[d, j * share : (j + 1) * share, :] = laid[
                     d * share : (d + 1) * share, p * BCOLS : (p + 1) * BCOLS
                 ]
+        at = slice(pair[0] * share, (pair[-1] + 1) * share)
+        copies.append(
+            pltpu.make_async_copy(piece.at[:, at], out_ref.at[:, at], sem.at[len(copies)])
+        )
+        copies[-1].start()
+    for copy in copies:
+        copy.wait()
 
 
 def columns_of(block, kh, kl):
@@ -550,8 +558,12 @@
         functools.partial(large_kernel, first=part, **settings),
         out_shape=jax.ShapeDtypeStruct((sources, (per - part) * share, BCOLS), f32),
         in_specs=vmem(5),
-        out_specs=pl.BlockSpec(memory_space=pltpu.VMEM),
-        scratch_shapes=[pltpu.VMEM((per - part, rows, width), f32)],
+        out_specs=pl.BlockSpec(memory_space=pltpu.HBM),
+        scratch_shapes=[
+            pltpu.VMEM((per - part, rows, width), f32),
+            pltpu.VMEM((sources, (per - part) * share, BCOLS), f32),
+            pltpu.SemaphoreType.DMA((per - part,)),
+        ],
         compiler_params=params(20),
         name="correct1",
     )

time: 78.4 us -> 78.3 us (level)
  no operation moved by 1% of the time
where the time goes in v4:
time: 78.3 us; the launch traced here: 77.9 us
  waiting for transfers between devices  42.9 us (55%)
  starting transfers between devices  24.4 us (31%)
  Pallas kernels  8.56 us (11%)
  local copies, waits for them, and re-layouts  1.92 us (2%)
    ppermute x6, waiting for transfers between devices, local(): lax.ppermute(small[d], 'space', [(i, i ^ d) for i in range(spaces)])  28.5 us
    ppermute x6, waiting for transfers between devices, across_sides(): received.append(lax.ppermute(pieces[k], ('date', 'band'), pairs))  14.4 us
    ppermute x6, starting transfers between devices, local(): lax.ppermute(small[d], 'space', [(i, i ^ d) for i in range(spaces)])  8.98 us
    all_to_all x1, starting transfers between devices, local(): lax.all_to_all(rest, 'space', split_axis=0, concat_axis=0, tiled=True)  6.35 us
    all_to_all x1, starting transfers between devices, local(): lax.all_to_all(laid, ('space', 'date', 'band'), split_axis=0, concat_axis...  4.87 us
    ppermute x6, starting transfers between devices, across_sides(): received.append(lax.ppermute(pieces[k], ('date', 'band'), pairs))  4.25 us
    pallas_call x1, Pallas kernels, local(): laid = correct_large(large, lines, gains, ah, al)  2.71 us
    pallas_call x1, Pallas kernels, local(): *sides, ah, al = correct_small(lines, gains, *small)  2.03 us
  transfers between devices with their start and end apart: 14, of which 7 were waited for; matrix products, arithmetic and copies ran while one was open for 0% of the time, Pallas kernels for 4%

profile of v4, /device:TPU:0, one launch (start us, length us, event | category | flops | bytes accessed | tf_op | source)
XLA Modules:
  0.0 77.9 jit_solution(11871350140269005285)
XLA Ops:
  0.0 0.0 copy-start
  0.0 1.2 %copy-done = f32[8,4,32,256]{3,2,1,0:T(8,128)S(1)} copy-done((f32[8,4,32,256]{3,2,1,0:T(8,128)S(1)}, f32[8,4,32,256]{3,2,1,0:T(8,128)}, u32[]{:S(2)}) %copy-start) | copy-done | bytes 1048600
  1.2 0.8 %cut.1 = f32[4,4,32,256]{3,2,1,0:T(8,128)} custom-call(f32[4,8,32,256]{3,2,1,0:T(8,128)S(1)} %bitcast.4), custom_call_target="tpu_custom_call" | custom-call | tf_op jit(solution)/shard_map/cut/pallas_call | solution.py:492
  2.1 6.3 %all-to-all-start = ((f32[4,4,32,256]{3,2,1,0:T(8,128)}), f32[4,4,32,256]{3,2,1,0:T(8,128)S(1)}, u32[]{:S(2)}, u32[]{:S(2)}) async-start(f32[4,4,32,256]{3,2,1,0:T(8,128)} %cut.1), calls=%async_computation | async-start | bytes 1048576 | tf_op jit(solution)/shard_map/all_to_all | solution.py:493
  8.4 0.0 copy-start.8
  8.4 0.0 copy-done.1
  8.5 0.7 copy-done.4
  9.1 0.0 copy-done.6
  9.1 0.0 copy-done.7
  9.1 0.0 copy-done.8
  9.1 0.2 pack.1
  9.3 0.0 copy-start.5
  9.3 2.1 %collective-permute-start = (f32[136,256]{1,0:T(8,128)S(1)}, f32[136,256]{1,0:T(8,128)S(1)}, u32[]{:S(2)}, u32[]{:S(2)}) collective-permute-start(f32[136,256]{1,0:T(8,128)S(1)} %get-tuple-element.33), channel_id=1, source_target_pairs={{0,4},{4,0},{8,12},{12,8},{1,5},{5,1},{9,13},{13,9},{2,6},{6,2},{1... | collective-permute-start | bytes 417800 | tf_op jit(solution)/shard_map/ppermute | solution.py:483
  11.4 2.4 %collective-permute-start.1 = (f32[136,256]{1,0:T(8,128)S(1)}, f32[136,256]{1,0:T(8,128)S(1)}, u32[]{:S(2)}, u32[]{:S(2)}) collective-permute-start(f32[136,256]{1,0:T(8,128)S(1)} %get-tuple-element.34), channel_id=1, source_target_pairs={{0,8},{4,12},{8,0},{12,4},{1,9},{5,13},{9,1},{13,5},{2,10},{6,14},... | collective-permute-start | bytes 417800 | tf_op jit(solution)/shard_map/ppermute | solution.py:483
  13.8 0.1 collective-permute-start.2
  13.9 0.0 copy-done.3
  13.9 0.0 copy-done.5
  13.9 0.3 taps.1
  14.2 7.0 %collective-permute-done.refs_1_ = f32[136,256]{1,0:T(8,128)S(1)} collective-permute-done((f32[136,256]{1,0:T(8,128)S(1)}, f32[136,256]{1,0:T(8,128)S(1)}, u32[]{:S(2)}, u32[]{:S(2)}) %collective-permute-start) | collective-permute-done | bytes 139296 | tf_op jit(solution)/shard_map/ppermute | solution.py:483
  21.2 11.7 %collective-permute-done.1.refs_2_ = f32[136,256]{1,0:T(8,128)S(1)} collective-permute-done((f32[136,256]{1,0:T(8,128)S(1)}, f32[136,256]{1,0:T(8,128)S(1)}, u32[]{:S(2)}, u32[]{:S(2)}) %collective-permute-start.1) | collective-permute-done | bytes 139296 | tf_op jit(solution)/shard_map/ppermute | solution.py:483
  32.9 0.0 collective-permute-done.2.refs_3_
  32.9 2.0 %correct0.1 = (f32[4,72,128]{2,1,0:T(8,128)S(1)}, f32[4,72,128]{2,1,0:T(8,128)S(1)}, f32[4,72,128]{2,1,0:T(8,128)S(1)}, f32[4,72,128]{2,1,0:T(8,128)S(1)}, bf16[...) custom-call(f32[2,12,384]{2,1,0:T(8,128)S(1)} %get-tuple-element.30.line_ref, ...), custom_call_target="tpu_custom_call" | custom-call | tf_op jit(solution)/shard_map/correct0/pallas_call | solution.py:542
  34.9 0.0 all-to-all-done.x_ref
  34.9 2.7 %correct1.1 = f32[16,64,128]{2,1,0:T(8,128)} custom-call(f32[4,4,32,256]{3,2,1,0:T(8,128)S(1)} %all-to-all-done.x_ref, f32[2,12,384]{2,1,0:T(8,128)S(1)} %get-tuple-element.30.line_ref, f32[12,256]{1,0:T(8,128)S(1)} %get-tuple-element.31.gain_ref, bf16[256,256]{1,0:T(8,128)(2,1)S(1)} %get-tuple-element.47.ah_ref, bf16[256,256]{1,0:T(8,128)(2,1)S(1)} %get-tuple-element.48.al_ref), custom_call_target="tpu_custom_call" | custom-call | tf_op jit(solution)/shard_map/correct1/pallas_call | solution.py:570
  37.6 4.9 %all-to-all-start.1 = ((f32[16,64,128]{2,1,0:T(8,128)}), f32[16,64,128]{2,1,0:T(8,128)S(1)}, u32[]{:S(2)}, u32[]{:S(2)}) async-start(f32[16,64,128]{2,1,0:T(8,128)} %correct1.1), calls=%async_computation.1 | async-start | bytes 1048576 | tf_op jit(solution)/shard_map/all_to_all | solution.py:571
  42.5 0.4 collective-permute-start.3
  42.9 1.6 %collective-permute-start.4 = (f32[4,72,128]{2,1,0:T(8,128)S(1)}, f32[4,72,128]{2,1,0:T(8,128)S(1)}, u32[]{:S(2)}, u32[]{:S(2)}) collective-permute-start(f32[4,72,128]{2,1,0:T(8,128)S(1)} %get-tuple-element.38), channel_id=1, source_target_pairs={{0,2},{1,3},{2,0},{3,1},{4,6},{5,7},{6,4},{7,5},{8,10},{9,11},{10,... | collective-permute-start | bytes 442376 | tf_op jit(solution)/shard_map/ppermute | solution.py:431
  44.5 0.0 collective-permute-start.5
  44.5 0.0 collective-permute-done.3.refs_1_
  44.5 9.0 %collective-permute-done.4.refs_2_ = f32[4,72,128]{2,1,0:T(8,128)S(1)} collective-permute-done((f32[4,72,128]{2,1,0:T(8,128)S(1)}, f32[4,72,128]{2,1,0:T(8,128)S(1)}, u32[]{:S(2)}, u32[]{:S(2)}) %collective-permute-start.4) | collective-permute-done | bytes 147488 | tf_op jit(solution)/shard_map/ppermute | solution.py:431
  53.6 3.2 %collective-permute-done.5.refs_3_ = f32[4,72,128]{2,1,0:T(8,128)S(1)} collective-permute-done((f32[4,72,128]{2,1,0:T(8,128)S(1)}, f32[4,72,128]{2,1,0:T(8,128)S(1)}, u32[]{:S(2)}, u32[]{:S(2)}) %collective-permute-start.5) | collective-permute-done | bytes 147488 | tf_op jit(solution)/shard_map/ppermute | solution.py:431
  56.8 1.3 %collective-permute-start.6 = (f32[4,64,128]{2,1,0:T(8,128)S(1)}, f32[4,64,128]{2,1,0:T(8,128)S(1)}, u32[]{:S(2)}, u32[]{:S(2)}) collective-permute-start(f32[4,64,128]{2,1,0:T(8,128)S(1)} %get-tuple-element.42), channel_id=1, source_target_pairs={{0,4},{4,0},{8,12},{12,8},{1,5},{5,1},{9,13},{13,9},{2,6},{6,2},{1... | collective-permute-start | bytes 393224 | tf_op jit(solution)/shard_map/ppermute | solution.py:555
  58.2 2.8 %collective-permute-start.7 = (f32[4,64,128]{2,1,0:T(8,128)S(1)}, f32[4,64,128]{2,1,0:T(8,128)S(1)}, u32[]{:S(2)}, u32[]{:S(2)}) collective-permute-start(f32[4,64,128]{2,1,0:T(8,128)S(1)} %get-tuple-element.43), channel_id=1, source_target_pairs={{0,8},{4,12},{8,0},{12,4},{1,9},{5,13},{9,1},{13,5},{2,10},{6,14},... | collective-permute-start | bytes 393224 | tf_op jit(solution)/shard_map/ppermute | solution.py:555
  61.0 0.3 collective-permute-start.8
  61.3 0.0 copy-done.2
  61.3 3.9 %collective-permute-done.6.refs_1_ = f32[4,64,128]{2,1,0:T(8,128)S(1)} collective-permute-done((f32[4,64,128]{2,1,0:T(8,128)S(1)}, f32[4,64,128]{2,1,0:T(8,128)S(1)}, u32[]{:S(2)}, u32[]{:S(2)}) %collective-permute-start.6) | collective-permute-done | bytes 131104 | tf_op jit(solution)/shard_map/ppermute | solution.py:555
  65.2 5.9 %collective-permute-done.7.refs_2_ = f32[4,64,128]{2,1,0:T(8,128)S(1)} collective-permute-done((f32[4,64,128]{2,1,0:T(8,128)S(1)}, f32[4,64,128]{2,1,0:T(8,128)S(1)}, u32[]{:S(2)}, u32[]{:S(2)}) %collective-permute-start.7) | collective-permute-done | bytes 131104 | tf_op jit(solution)/shard_map/ppermute | solution.py:555
  71.1 0.0 collective-permute-done.8.refs_3_
  71.1 0.4 columns.1
  71.5 0.0 all-to-all-done.1.y_ref
  71.5 1.4 %median.1 = (f32[4,16,128]{2,1,0:T(8,128)S(1)}, f32[4,16,128]{2,1,0:T(8,128)S(1)}) custom-call(f32[16,8,128]{2,1,0:T(8,128)S(1)} %get-tuple-element.45.weight_ref, bf16[128,128]{1,0:T(8,128)(2,1)S(1)} %get-tuple-element.28.kh_ref, bf16[128,128]{1,0:T(8,128)(2,1)S(1)} %get-tuple-element.29.kl_ref, f32[4,4,4,16,128]{4,3,2,1,0:T(8,128)S(1)} %get-tuple-element.46.small_ref, ...), custom_call_target="tpu_custom_call" | custom-call | tf_op jit(solution)/shard_map/median/pallas_call | solution.py:598
  72.9 0.6 collective-permute-start.10
  73.5 0.0 collective-permute-start.11
  73.5 1.6 %collective-permute-start.9 = (f32[4,16,128]{2,1,0:T(8,128)S(1)}, f32[4,16,128]{2,1,0:T(8,128)S(1)}, u32[]{:S(2)}, u32[]{:S(2)}) collective-permute-start(f32[4,16,128]{2,1,0:T(8,128)S(1)} %get-tuple-element.50), channel_id=1, source_target_pairs={{0,1},{1,0},{2,3},{3,2},{4,5},{5,4},{6,7},{7,6},{8,9},{9,8},{10,11... | collective-permute-start | bytes 98312 | tf_op jit(solution)/shard_map/ppermute | solution.py:431
  75.1 2.1 %collective-permute-done.10.refs_2_ = f32[4,16,128]{2,1,0:T(8,128)S(1)} collective-permute-done((f32[4,16,128]{2,1,0:T(8,128)S(1)}, f32[4,16,128]{2,1,0:T(8,128)S(1)}, u32[]{:S(2)}, u32[]{:S(2)}) %collective-permute-start.10) | collective-permute-done | bytes 32800 | tf_op jit(solution)/shard_map/ppermute | solution.py:431
  77.2 0.0 collective-permute-done.11.refs_3_
  77.2 0.0 collective-permute-done.9.refs_1_
  77.2 0.7 place.1
  (8 shorter events, 0.1 us)
Async XLA Ops:
  0.0 1.2 %copy-start = (f32[8,4,32,256]{3,2,1,0:T(8,128)S(1)}, f32[8,4,32,256]{3,2,1,0:T(8,128)}, u32[]{:S(2)}) copy-start(f32[8,4,32,256]{3,2,1,0:T(8,128)} %param.8) | copy-start | bytes 3145732
  1.2 7.2 %copy-start.1 = (f32[8,4,32,256]{3,2,1,0:T(8,128)S(1)}, f32[8,4,32,256]{3,2,1,0:T(8,128)}, u32[]{:S(2)}) copy-start(f32[8,4,32,256]{3,2,1,0:T(8,128)} %param.8) | copy-start | bytes 3145732
  2.1 32.8 %all-to-all-start = ((f32[4,4,32,256]{3,2,1,0:T(8,128)}), f32[4,4,32,256]{3,2,1,0:T(8,128)S(1)}, u32[]{:S(2)}, u32[]{:S(2)}) async-start(f32[4,4,32,256]{3,2,1,0:T(8,128)} %cut.1), calls=%async_computation | async-start | bytes 1048576 | tf_op jit(solution)/shard_map/all_to_all | solution.py:493
  8.4 0.7 copy-start.4
  8.4 0.7 copy-start.6
  8.4 0.7 copy-start.7
  8.4 0.7 copy-start.8
  9.1 4.8 %copy-start.3 = (f32[3,4,33]{2,1,0:T(4,128)S(1)}, f32[3,4,33]{2,1,0:T(4,128)}, u32[]{:S(2)}) copy-start(f32[3,4,33]{2,1,0:T(4,128)} %kernels_hbm.1) | copy-start | bytes 4756
  9.3 4.5 %copy-start.5 = (f32[3,4]{1,0:T(4,128)S(1)}, f32[3,4]{1,0:T(4,128)}, u32[]{:S(2)}) copy-start(f32[3,4]{1,0:T(4,128)} %strength_hbm.1) | copy-start | bytes 148
  9.3 11.8 %collective-permute-start = (f32[136,256]{1,0:T(8,128)S(1)}, f32[136,256]{1,0:T(8,128)S(1)}, u32[]{:S(2)}, u32[]{:S(2)}) collective-permute-start(f32[136,256]{1,0:T(8,128)S(1)} %get-tuple-element.33), channel_id=1, source_target_pairs={{0,4},{4,0},{8,12},{12,8},{1,5},{5,1},{9,13},{13,9},{2,6},{6,2},{1... | collective-permute-start | bytes 417800 | tf_op jit(solution)/shard_map/ppermute | solution.py:483
  11.4 21.4 %collective-permute-start.1 = (f32[136,256]{1,0:T(8,128)S(1)}, f32[136,256]{1,0:T(8,128)S(1)}, u32[]{:S(2)}, u32[]{:S(2)}) collective-permute-start(f32[136,256]{1,0:T(8,128)S(1)} %get-tuple-element.34), channel_id=1, source_target_pairs={{0,8},{4,12},{8,0},{12,4},{1,9},{5,13},{9,1},{13,5},{2,10},{6,14},... | collective-permute-start | bytes 417800 | tf_op jit(solution)/shard_map/ppermute | solution.py:483
  13.8 19.1 %collective-permute-start.2 = (f32[136,256]{1,0:T(8,128)S(1)}, f32[136,256]{1,0:T(8,128)S(1)}, u32[]{:S(2)}, u32[]{:S(2)}) collective-permute-start(f32[136,256]{1,0:T(8,128)S(1)} %get-tuple-element.35), channel_id=1, source_target_pairs={{0,12},{4,8},{8,4},{12,0},{1,13},{5,9},{9,5},{13,1},{2,14},{6,10},... | collective-permute-start | bytes 417800 | tf_op jit(solution)/shard_map/ppermute | solution.py:483
  37.6 33.9 %all-to-all-start.1 = ((f32[16,64,128]{2,1,0:T(8,128)}), f32[16,64,128]{2,1,0:T(8,128)S(1)}, u32[]{:S(2)}, u32[]{:S(2)}) async-start(f32[16,64,128]{2,1,0:T(8,128)} %correct1.1), calls=%async_computation.1 | async-start | bytes 1048576 | tf_op jit(solution)/shard_map/all_to_all | solution.py:571
  42.5 2.0 %collective-permute-start.3 = (f32[4,72,128]{2,1,0:T(8,128)S(1)}, f32[4,72,128]{2,1,0:T(8,128)S(1)}, u32[]{:S(2)}, u32[]{:S(2)}) collective-permute-start(f32[4,72,128]{2,1,0:T(8,128)S(1)} %get-tuple-element.37), channel_id=1, source_target_pairs={{0,1},{1,0},{2,3},{3,2},{4,5},{5,4},{6,7},{7,6},{8,9},{9,8},{10,11... | collective-permute-start | bytes 442376 | tf_op jit(solution)/shard_map/ppermute | solution.py:431
  42.9 10.7 %collective-permute-start.4 = (f32[4,72,128]{2,1,0:T(8,128)S(1)}, f32[4,72,128]{2,1,0:T(8,128)S(1)}, u32[]{:S(2)}, u32[]{:S(2)}) collective-permute-start(f32[4,72,128]{2,1,0:T(8,128)S(1)} %get-tuple-element.38), channel_id=1, source_target_pairs={{0,2},{1,3},{2,0},{3,1},{4,6},{5,7},{6,4},{7,5},{8,10},{9,11},{10,... | collective-permute-start | bytes 442376 | tf_op jit(solution)/shard_map/ppermute | solution.py:431
  44.5 12.3 %collective-permute-start.5 = (f32[4,72,128]{2,1,0:T(8,128)S(1)}, f32[4,72,128]{2,1,0:T(8,128)S(1)}, u32[]{:S(2)}, u32[]{:S(2)}) collective-permute-start(f32[4,72,128]{2,1,0:T(8,128)S(1)} %get-tuple-element.39), channel_id=1, source_target_pairs={{0,3},{1,2},{2,1},{3,0},{4,7},{5,6},{6,5},{7,4},{8,11},{9,10},{10,... | collective-permute-start | bytes 442376 | tf_op jit(solution)/shard_map/ppermute | solution.py:431
  56.8 4.5 %copy-start.2 = (f32[1,128,128]{2,1,0:T(8,128)S(1)}, f32[1,128,128]{2,1,0:T(8,128)}, u32[]{:S(2)}) copy-start(f32[1,128,128]{2,1,0:T(8,128)} %cols_ref.1) | copy-start | bytes 196612
  56.8 8.4 %collective-permute-start.6 = (f32[4,64,128]{2,1,0:T(8,128)S(1)}, f32[4,64,128]{2,1,0:T(8,128)S(1)}, u32[]{:S(2)}, u32[]{:S(2)}) collective-permute-start(f32[4,64,128]{2,1,0:T(8,128)S(1)} %get-tuple-element.42), channel_id=1, source_target_pairs={{0,4},{4,0},{8,12},{12,8},{1,5},{5,1},{9,13},{13,9},{2,6},{6,2},{1... | collective-permute-start | bytes 393224 | tf_op jit(solution)/shard_map/ppermute | solution.py:555
  58.2 12.9 %collective-permute-start.7 = (f32[4,64,128]{2,1,0:T(8,128)S(1)}, f32[4,64,128]{2,1,0:T(8,128)S(1)}, u32[]{:S(2)}, u32[]{:S(2)}) collective-permute-start(f32[4,64,128]{2,1,0:T(8,128)S(1)} %get-tuple-element.43), channel_id=1, source_target_pairs={{0,8},{4,12},{8,0},{12,4},{1,9},{5,13},{9,1},{13,5},{2,10},{6,14},... | collective-permute-start | bytes 393224 | tf_op jit(solution)/shard_map/ppermute | solution.py:555
  61.0 10.1 %collective-permute-start.8 = (f32[4,64,128]{2,1,0:T(8,128)S(1)}, f32[4,64,128]{2,1,0:T(8,128)S(1)}, u32[]{:S(2)}, u32[]{:S(2)}) collective-permute-start(f32[4,64,128]{2,1,0:T(8,128)S(1)} %get-tuple-element.44), channel_id=1, source_target_pairs={{0,12},{4,8},{8,4},{12,0},{1,13},{5,9},{9,5},{13,1},{2,14},{6,10},... | collective-permute-start | bytes 393224 | tf_op jit(solution)/shard_map/ppermute | solution.py:555
  72.9 4.3 %collective-permute-start.10 = (f32[4,16,128]{2,1,0:T(8,128)S(1)}, f32[4,16,128]{2,1,0:T(8,128)S(1)}, u32[]{:S(2)}, u32[]{:S(2)}) collective-permute-start(f32[4,16,128]{2,1,0:T(8,128)S(1)} %get-tuple-element.49.refs_0_), channel_id=1, source_target_pairs={{0,2},{1,3},{2,0},{3,1},{4,6},{5,7},{6,4},{7,5},{8,10},{9,11},{10,... | collective-permute-start | bytes 98312 | tf_op jit(solution)/shard_map/ppermute | solution.py:431
  73.5 3.7 %collective-permute-start.11 = (f32[4,16,128]{2,1,0:T(8,128)S(1)}, f32[4,16,128]{2,1,0:T(8,128)S(1)}, u32[]{:S(2)}, u32[]{:S(2)}) collective-permute-start(f32[4,16,128]{2,1,0:T(8,128)S(1)} %get-tuple-element.50), channel_id=1, source_target_pairs={{0,3},{1,2},{2,1},{3,0},{4,7},{5,6},{6,5},{7,4},{8,11},{9,10},{10,... | collective-permute-start | bytes 98312 | tf_op jit(solution)/shard_map/ppermute | solution.py:431
  73.5 3.7 %collective-permute-start.9 = (f32[4,16,128]{2,1,0:T(8,128)S(1)}, f32[4,16,128]{2,1,0:T(8,128)S(1)}, u32[]{:S(2)}, u32[]{:S(2)}) collective-permute-start(f32[4,16,128]{2,1,0:T(8,128)S(1)} %get-tuple-element.50), channel_id=1, source_target_pairs={{0,1},{1,0},{2,3},{3,2},{4,5},{5,4},{6,7},{7,6},{8,9},{9,8},{10,11... | collective-permute-start | bytes 98312 | tf_op jit(solution)/shard_map/ppermute | solution.py:431

commit v5 on v4

--- a/solution.py
+++ b/solution.py
@@ -248,6 +248,7 @@
     corrections(state, line_ref, gain_ref, 0, passes, bands, radius)
     x, c = lax.axis_index("date"), lax.axis_index("band")
     groups = laid_ref.shape[0]
+    unit = out_refs[0].shape[1]
     for pair, laid in laid_pairs(state, ah, al):
         for m in range(groups):
             laid_ref[m, :, : laid.shape[1]] = laid[m * share : (m + 1) * share]
@@ -256,14 +257,16 @@
             for g in range(spaces):
                 lines = laid_ref[g * (groups // spaces) + mine]
                 for p, j in enumerate(pair):
-                    out[g, j * share : (j + 1) * share, :] = lines[
-                        :, p * BCOLS : (p + 1) * BCOLS
-                    ]
+                    for r in range(0, share, unit):
+                        out[(g * part * share + j * share + r) // unit] = lines[
+                            r : r + unit, p * BCOLS : (p + 1) * BCOLS
+                        ]
     at = tables + BROWS + 2 * table_lines
     counted = [ref[at : at + 1, 0:BCOLS] for ref in x_refs]
     for out in out_refs:
-        out[0, part * share : part * share + 1, :] = counted[0]
-        out[0, part * share + 1 : part * share + 2, :] = total(counted)
+        out[out.shape[0] - 1] = jnp.concatenate(
+            [counted[0], total(counted)] + [jnp.zeros_like(counted[0])] * (unit - 2), axis=0
+        )
 
 
 def large_kernel(
@@ -303,11 +306,15 @@
 
 def regroup_kernel(*refs, spaces):
     groups, size = refs[-2].shape[:2]
+    unit = refs[0].shape[1]
     own = lax.axis_index("space")
     for k in range(groups):
         for d in range(spaces):
-            refs[groups + d][k] = refs[k][own ^ d, :size, :]
-        refs[-1][k] = refs[k][0, size:, :]
+            for r in range(0, size, unit):
+                refs[groups + d][k, r : r + unit, :] = refs[k][
+                    (own ^ d) * (size // unit) + r // unit
+                ]
+        refs[-1][k] = refs[k][refs[k].shape[0] - 1]
 
 
 def columns_kernel(
@@ -448,7 +455,7 @@
     share = tile_rows // (dates * cores)
     tile = min(share, SUBLANES)
     per = local_dates * bands // spaces
-    part = max(1, per // 2)
+    part = max(1, per * 3 // 8)
     images = reflect.reshape(spaces, per, strip, width)
     pack = pl.pallas_call(
         functools.partial(pack_kernel, part=part, halves=halves, table_lines=table_lines),
@@ -518,7 +525,8 @@
     lines, gains = make_lines(kernels, strength)
 
     settings = dict(passes=passes, bands=here, radius=kernels.shape[2] // 2)
-    small_rows = part * share + SUBLANES
+    unit = min(share, SUBLANES)
+    small_blocks = spaces * part * share // unit + 1
     correct_small = pl.pallas_call(
         functools.partial(
             small_kernel,
@@ -528,7 +536,7 @@
             table_lines=table_lines,
             **settings,
         ),
-        out_shape=[jax.ShapeDtypeStruct((spaces, small_rows, BCOLS), f32)] * (dates * cores)
+        out_shape=[jax.ShapeDtypeStruct((small_blocks, unit, BCOLS), f32)] * (dates * cores)
         + [jax.ShapeDtypeStruct((spaces * tile_rows, length), bf16)] * 2,
         in_specs=vmem(2 + spaces),
         out_specs=vmem(dates * cores + 2),
@@ -544,7 +552,7 @@
     regroup = pl.pallas_call(
         functools.partial(regroup_kernel, spaces=spaces),
         out_shape=[jax.ShapeDtypeStruct((dates * cores, part * share, BCOLS), f32)] * spaces
-        + [jax.ShapeDtypeStruct((dates * cores, SUBLANES, BCOLS), f32)],
+        + [jax.ShapeDtypeStruct((dates * cores, unit, BCOLS), f32)],
         in_specs=vmem(dates * cores),
         out_specs=vmem(spaces + 1),
         compiler_params=params(4),

time: 78.3 us -> 75.5 us (0.964)
  waiting for transfers between devices: 42.9 us -> 40.1 us
    ppermute x6, waiting for transfers between devices: 14.4 us -> 12.8 us  [across_sides(): received.append(lax.ppermute(pieces[k], ('date', 'band'), pairs))]
    ppermute x6, waiting for transfers between devices: 28.5 us -> 27.3 us  [local(): lax.ppermute(small[d], 'space', [(i, i ^ d) for i in range(spaces)])]
  transfers between devices with their start and end apart: 14 -> 14, of which waited for: 7 -> 8; matrix products, arithmetic and copies ran while one was open for 0% -> 0% of each run, Pallas kernels for 4% -> 3%
where the time goes in v5:
time: 75.5 us; the launch traced here: 75.2 us
  waiting for transfers between devices  40.1 us (53%)
  starting transfers between devices  24.2 us (32%)
  Pallas kernels  8.76 us (12%)
  local copies, waits for them, and re-layouts  1.92 us (3%)
    ppermute x6, waiting for transfers between devices, local(): lax.ppermute(small[d], 'space', [(i, i ^ d) for i in range(spaces)])  27.3 us
    ppermute x6, waiting for transfers between devices, across_sides(): received.append(lax.ppermute(pieces[k], ('date', 'band'), pairs))  12.8 us
    ppermute x6, starting transfers between devices, local(): lax.ppermute(small[d], 'space', [(i, i ^ d) for i in range(spaces)])  9.34 us
    all_to_all x1, starting transfers between devices, local(): lax.all_to_all(rest, 'space', split_axis=0, concat_axis=0, tiled=True)  6.48 us
    ppermute x6, starting transfers between devices, across_sides(): received.append(lax.ppermute(pieces[k], ('date', 'band'), pairs))  4.25 us
    all_to_all x1, starting transfers between devices, local(): lax.all_to_all(laid, ('space', 'date', 'band'), split_axis=0, concat_axis...  4.16 us
    pallas_call x1, Pallas kernels, local(): laid = correct_large(large, lines, gains, ah, al)  3.07 us
    unnamed x18, local copies, waits for them, and re-layouts  1.92 us
  transfers between devices with their start and end apart: 14, of which 8 were waited for; matrix products, arithmetic and copies ran while one was open for 0% of the time, Pallas kernels for 3%

profile of v5, /device:TPU:0, one launch (start us, length us, event | category | flops | bytes accessed | tf_op | source)
XLA Modules:
  0.0 75.2 jit_solution(8659677938751322045)
XLA Ops:
  0.0 0.0 copy-start
  0.0 1.2 %copy-done = f32[8,4,32,256]{3,2,1,0:T(8,128)S(1)} copy-done((f32[8,4,32,256]{3,2,1,0:T(8,128)S(1)}, f32[8,4,32,256]{3,2,1,0:T(8,128)}, u32[]{:S(2)}) %copy-start) | copy-done | bytes 1048600
  1.2 0.9 %cut.1 = f32[4,5,32,256]{3,2,1,0:T(8,128)} custom-call(f32[4,8,32,256]{3,2,1,0:T(8,128)S(1)} %bitcast.4), custom_call_target="tpu_custom_call" | custom-call | tf_op jit(solution)/shard_map/cut/pallas_call | solution.py:499
  2.1 6.5 %all-to-all-start = ((f32[4,5,32,256]{3,2,1,0:T(8,128)}), f32[4,5,32,256]{3,2,1,0:T(8,128)S(1)}, u32[]{:S(2)}, u32[]{:S(2)}) async-start(f32[4,5,32,256]{3,2,1,0:T(8,128)} %cut.1), calls=%async_computation | async-start | bytes 1310720 | tf_op jit(solution)/shard_map/all_to_all | solution.py:500
  8.6 0.0 copy-start.8
  8.6 0.0 copy-done.1
  8.6 0.7 copy-done.4
  9.3 0.0 copy-done.6
  9.3 0.0 copy-done.7
  9.3 0.0 copy-done.8
  9.3 0.2 pack.1
  9.5 0.0 copy-start.5
  9.5 2.1 %collective-permute-start = (f32[104,256]{1,0:T(8,128)S(1)}, f32[104,256]{1,0:T(8,128)S(1)}, u32[]{:S(2)}, u32[]{:S(2)}) collective-permute-start(f32[104,256]{1,0:T(8,128)S(1)} %get-tuple-element.33), channel_id=1, source_target_pairs={{0,4},{4,0},{8,12},{12,8},{1,5},{5,1},{9,13},{13,9},{2,6},{6,2},{1... | collective-permute-start | bytes 319496 | tf_op jit(solution)/shard_map/ppermute | solution.py:490
  11.6 2.4 %collective-permute-start.1 = (f32[104,256]{1,0:T(8,128)S(1)}, f32[104,256]{1,0:T(8,128)S(1)}, u32[]{:S(2)}, u32[]{:S(2)}) collective-permute-start(f32[104,256]{1,0:T(8,128)S(1)} %get-tuple-element.34), channel_id=1, source_target_pairs={{0,8},{4,12},{8,0},{12,4},{1,9},{5,13},{9,1},{13,5},{2,10},{6,14},... | collective-permute-start | bytes 319496 | tf_op jit(solution)/shard_map/ppermute | solution.py:490
  13.9 0.1 collective-permute-start.2
  14.0 0.0 copy-done.3
  14.0 0.0 copy-done.5
  14.0 0.3 taps.1
  14.3 8.4 %collective-permute-done.refs_1_ = f32[104,256]{1,0:T(8,128)S(1)} collective-permute-done((f32[104,256]{1,0:T(8,128)S(1)}, f32[104,256]{1,0:T(8,128)S(1)}, u32[]{:S(2)}, u32[]{:S(2)}) %collective-permute-start) | collective-permute-done | bytes 106528 | tf_op jit(solution)/shard_map/ppermute | solution.py:490
  22.7 11.0 %collective-permute-done.1.refs_2_ = f32[104,256]{1,0:T(8,128)S(1)} collective-permute-done((f32[104,256]{1,0:T(8,128)S(1)}, f32[104,256]{1,0:T(8,128)S(1)}, u32[]{:S(2)}, u32[]{:S(2)}) %collective-permute-start.1) | collective-permute-done | bytes 106528 | tf_op jit(solution)/shard_map/ppermute | solution.py:490
  33.7 0.0 collective-permute-done.2.refs_3_
  33.7 1.8 %correct0.1 = (f32[25,8,128]{2,1,0:T(8,128)S(1)}, f32[25,8,128]{2,1,0:T(8,128)S(1)}, f32[25,8,128]{2,1,0:T(8,128)S(1)}, f32[25,8,128]{2,1,0:T(8,128)S(1)}, bf16[...) custom-call(f32[2,12,384]{2,1,0:T(8,128)S(1)} %get-tuple-element.30.line_ref, ...), custom_call_target="tpu_custom_call" | custom-call | tf_op jit(solution)/shard_map/correct0/pallas_call | solution.py:550
  35.5 0.0 all-to-all-done.x_ref
  35.5 3.1 %correct1.1 = f32[16,80,128]{2,1,0:T(8,128)} custom-call(f32[4,5,32,256]{3,2,1,0:T(8,128)S(1)} %all-to-all-done.x_ref, f32[2,12,384]{2,1,0:T(8,128)S(1)} %get-tuple-element.30.line_ref, f32[12,256]{1,0:T(8,128)S(1)} %get-tuple-element.31.gain_ref, bf16[256,256]{1,0:T(8,128)(2,1)S(1)} %get-tuple-element.47.ah_ref, bf16[256,256]{1,0:T(8,128)(2,1)S(1)} %get-tuple-element.48.al_ref), custom_call_target="tpu_custom_call" | custom-call | tf_op jit(solution)/shard_map/correct1/pallas_call | solution.py:578
  38.6 4.2 %all-to-all-start.1 = ((f32[16,80,128]{2,1,0:T(8,128)}), f32[16,80,128]{2,1,0:T(8,128)S(1)}, u32[]{:S(2)}, u32[]{:S(2)}) async-start(f32[16,80,128]{2,1,0:T(8,128)} %correct1.1), calls=%async_computation.1 | async-start | bytes 1310720 | tf_op jit(solution)/shard_map/all_to_all | solution.py:579
  42.8 0.4 collective-permute-start.3
  43.2 1.6 %collective-permute-start.4 = (f32[25,8,128]{2,1,0:T(8,128)S(1)}, f32[25,8,128]{2,1,0:T(8,128)S(1)}, u32[]{:S(2)}, u32[]{:S(2)}) collective-permute-start(f32[25,8,128]{2,1,0:T(8,128)S(1)} %get-tuple-element.38), channel_id=1, source_target_pairs={{0,2},{1,3},{2,0},{3,1},{4,6},{5,7},{6,4},{7,5},{8,10},{9,11},{10,... | collective-permute-start | bytes 307208 | tf_op jit(solution)/shard_map/ppermute | solution.py:438
  44.8 0.0 collective-permute-start.5
  44.8 0.0 collective-permute-done.3.refs_1_
  44.8 8.6 %collective-permute-done.4.refs_2_ = f32[25,8,128]{2,1,0:T(8,128)S(1)} collective-permute-done((f32[25,8,128]{2,1,0:T(8,128)S(1)}, f32[25,8,128]{2,1,0:T(8,128)S(1)}, u32[]{:S(2)}, u32[]{:S(2)}) %collective-permute-start.4) | collective-permute-done | bytes 102432 | tf_op jit(solution)/shard_map/ppermute | solution.py:438
  53.4 1.5 %collective-permute-done.5.refs_3_ = f32[25,8,128]{2,1,0:T(8,128)S(1)} collective-permute-done((f32[25,8,128]{2,1,0:T(8,128)S(1)}, f32[25,8,128]{2,1,0:T(8,128)S(1)}, u32[]{:S(2)}, u32[]{:S(2)}) %collective-permute-start.5) | collective-permute-done | bytes 102432 | tf_op jit(solution)/shard_map/ppermute | solution.py:438
  55.0 0.9 %collective-permute-start.6 = (f32[4,48,128]{2,1,0:T(8,128)S(1)}, f32[4,48,128]{2,1,0:T(8,128)S(1)}, u32[]{:S(2)}, u32[]{:S(2)}) collective-permute-start(f32[4,48,128]{2,1,0:T(8,128)S(1)} %get-tuple-element.42), channel_id=1, source_target_pairs={{0,4},{4,0},{8,12},{12,8},{1,5},{5,1},{9,13},{13,9},{2,6},{6,2},{1... | collective-permute-start | bytes 294920 | tf_op jit(solution)/shard_map/ppermute | solution.py:563
  55.8 3.9 %collective-permute-start.7 = (f32[4,48,128]{2,1,0:T(8,128)S(1)}, f32[4,48,128]{2,1,0:T(8,128)S(1)}, u32[]{:S(2)}, u32[]{:S(2)}) collective-permute-start(f32[4,48,128]{2,1,0:T(8,128)S(1)} %get-tuple-element.43), channel_id=1, source_target_pairs={{0,8},{4,12},{8,0},{12,4},{1,9},{5,13},{9,1},{13,5},{2,10},{6,14},... | collective-permute-start | bytes 294920 | tf_op jit(solution)/shard_map/ppermute | solution.py:563
  59.8 0.0 collective-permute-start.8
  59.8 0.0 copy-done.2
  59.8 3.0 %collective-permute-done.6.refs_1_ = f32[4,48,128]{2,1,0:T(8,128)S(1)} collective-permute-done((f32[4,48,128]{2,1,0:T(8,128)S(1)}, f32[4,48,128]{2,1,0:T(8,128)S(1)}, u32[]{:S(2)}, u32[]{:S(2)}) %collective-permute-start.6) | collective-permute-done | bytes 98336 | tf_op jit(solution)/shard_map/ppermute | solution.py:563
  62.8 4.9 %collective-permute-done.7.refs_2_ = f32[4,48,128]{2,1,0:T(8,128)S(1)} collective-permute-done((f32[4,48,128]{2,1,0:T(8,128)S(1)}, f32[4,48,128]{2,1,0:T(8,128)S(1)}, u32[]{:S(2)}, u32[]{:S(2)}) %collective-permute-start.7) | collective-permute-done | bytes 98336 | tf_op jit(solution)/shard_map/ppermute | solution.py:563
  67.7 0.0 collective-permute-done.8.refs_3_
  67.7 0.3 columns.1
  68.0 0.0 all-to-all-done.1.y_ref
  68.0 1.6 %median.1 = (f32[4,16,128]{2,1,0:T(8,128)S(1)}, f32[4,16,128]{2,1,0:T(8,128)S(1)}) custom-call(f32[16,8,128]{2,1,0:T(8,128)S(1)} %get-tuple-element.45.weight_ref, bf16[128,128]{1,0:T(8,128)(2,1)S(1)} %get-tuple-element.28.kh_ref, bf16[128,128]{1,0:T(8,128)(2,1)S(1)} %get-tuple-element.29.kl_ref, f32[4,4,3,16,128]{4,3,2,1,0:T(8,128)S(1)} %get-tuple-element.46.small_ref, ...), custom_call_target="tpu_custom_call" | custom-call | tf_op jit(solution)/shard_map/median/pallas_call | solution.py:606
  69.6 1.6 %collective-permute-start.10 = (f32[4,16,128]{2,1,0:T(8,128)S(1)}, f32[4,16,128]{2,1,0:T(8,128)S(1)}, u32[]{:S(2)}, u32[]{:S(2)}) collective-permute-start(f32[4,16,128]{2,1,0:T(8,128)S(1)} %get-tuple-element.49.refs_0_), channel_id=1, source_target_pairs={{0,2},{1,3},{2,0},{3,1},{4,6},{5,7},{6,4},{7,5},{8,10},{9,11},{10,... | collective-permute-start | bytes 98312 | tf_op jit(solution)/shard_map/ppermute | solution.py:438
  71.2 0.0 collective-permute-start.11
  71.2 0.6 collective-permute-start.9
  71.8 1.8 %collective-permute-done.10.refs_2_ = f32[4,16,128]{2,1,0:T(8,128)S(1)} collective-permute-done((f32[4,16,128]{2,1,0:T(8,128)S(1)}, f32[4,16,128]{2,1,0:T(8,128)S(1)}, u32[]{:S(2)}, u32[]{:S(2)}) %collective-permute-start.10) | collective-permute-done | bytes 32800 | tf_op jit(solution)/shard_map/ppermute | solution.py:438
  73.5 0.9 %collective-permute-done.11.refs_3_ = f32[4,16,128]{2,1,0:T(8,128)S(1)} collective-permute-done((f32[4,16,128]{2,1,0:T(8,128)S(1)}, f32[4,16,128]{2,1,0:T(8,128)S(1)}, u32[]{:S(2)}, u32[]{:S(2)}) %collective-permute-start.11) | collective-permute-done | bytes 32800 | tf_op jit(solution)/shard_map/ppermute | solution.py:438
  74.5 0.0 collective-permute-done.9.refs_1_
  74.5 0.7 place.1
  (8 shorter events, 0.0 us)
Async XLA Ops:
  0.0 1.2 %copy-start = (f32[8,4,32,256]{3,2,1,0:T(8,128)S(1)}, f32[8,4,32,256]{3,2,1,0:T(8,128)}, u32[]{:S(2)}) copy-start(f32[8,4,32,256]{3,2,1,0:T(8,128)} %param.8) | copy-start | bytes 3145732
  2.1 6.5 %copy-start.1 = (f32[8,4,32,256]{3,2,1,0:T(8,128)S(1)}, f32[8,4,32,256]{3,2,1,0:T(8,128)}, u32[]{:S(2)}) copy-start(f32[8,4,32,256]{3,2,1,0:T(8,128)} %param.8) | copy-start | bytes 3145732
  2.1 33.4 %all-to-all-start = ((f32[4,5,32,256]{3,2,1,0:T(8,128)}), f32[4,5,32,256]{3,2,1,0:T(8,128)S(1)}, u32[]{:S(2)}, u32[]{:S(2)}) async-start(f32[4,5,32,256]{3,2,1,0:T(8,128)} %cut.1), calls=%async_computation | async-start | bytes 1310720 | tf_op jit(solution)/shard_map/all_to_all | solution.py:500
  8.6 0.7 copy-start.4
  8.6 0.7 copy-start.6
  8.6 0.7 copy-start.7
  8.6 0.7 copy-start.8
  9.3 4.7 %copy-start.3 = (f32[3,4,33]{2,1,0:T(4,128)S(1)}, f32[3,4,33]{2,1,0:T(4,128)}, u32[]{:S(2)}) copy-start(f32[3,4,33]{2,1,0:T(4,128)} %kernels_hbm.1) | copy-start | bytes 4756
  9.5 4.5 %copy-start.5 = (f32[3,4]{1,0:T(4,128)S(1)}, f32[3,4]{1,0:T(4,128)}, u32[]{:S(2)}) copy-start(f32[3,4]{1,0:T(4,128)} %strength_hbm.1) | copy-start | bytes 148
  9.5 13.2 %collective-permute-start = (f32[104,256]{1,0:T(8,128)S(1)}, f32[104,256]{1,0:T(8,128)S(1)}, u32[]{:S(2)}, u32[]{:S(2)}) collective-permute-start(f32[104,256]{1,0:T(8,128)S(1)} %get-tuple-element.33), channel_id=1, source_target_pairs={{0,4},{4,0},{8,12},{12,8},{1,5},{5,1},{9,13},{13,9},{2,6},{6,2},{1... | collective-permute-start | bytes 319496 | tf_op jit(solution)/shard_map/ppermute | solution.py:490
  11.6 22.1 %collective-permute-start.1 = (f32[104,256]{1,0:T(8,128)S(1)}, f32[104,256]{1,0:T(8,128)S(1)}, u32[]{:S(2)}, u32[]{:S(2)}) collective-permute-start(f32[104,256]{1,0:T(8,128)S(1)} %get-tuple-element.34), channel_id=1, source_target_pairs={{0,8},{4,12},{8,0},{12,4},{1,9},{5,13},{9,1},{13,5},{2,10},{6,14},... | collective-permute-start | bytes 319496 | tf_op jit(solution)/shard_map/ppermute | solution.py:490
  13.9 19.8 %collective-permute-start.2 = (f32[104,256]{1,0:T(8,128)S(1)}, f32[104,256]{1,0:T(8,128)S(1)}, u32[]{:S(2)}, u32[]{:S(2)}) collective-permute-start(f32[104,256]{1,0:T(8,128)S(1)} %get-tuple-element.35), channel_id=1, source_target_pairs={{0,12},{4,8},{8,4},{12,0},{1,13},{5,9},{9,5},{13,1},{2,14},{6,10},... | collective-permute-start | bytes 319496 | tf_op jit(solution)/shard_map/ppermute | solution.py:490
  38.6 29.4 %all-to-all-start.1 = ((f32[16,80,128]{2,1,0:T(8,128)}), f32[16,80,128]{2,1,0:T(8,128)S(1)}, u32[]{:S(2)}, u32[]{:S(2)}) async-start(f32[16,80,128]{2,1,0:T(8,128)} %correct1.1), calls=%async_computation.1 | async-start | bytes 1310720 | tf_op jit(solution)/shard_map/all_to_all | solution.py:579
  42.8 2.0 %collective-permute-start.3 = (f32[25,8,128]{2,1,0:T(8,128)S(1)}, f32[25,8,128]{2,1,0:T(8,128)S(1)}, u32[]{:S(2)}, u32[]{:S(2)}) collective-permute-start(f32[25,8,128]{2,1,0:T(8,128)S(1)} %get-tuple-element.37), channel_id=1, source_target_pairs={{0,1},{1,0},{2,3},{3,2},{4,5},{5,4},{6,7},{7,6},{8,9},{9,8},{10,11... | collective-permute-start | bytes 307208 | tf_op jit(solution)/shard_map/ppermute | solution.py:438
  43.2 10.3 %collective-permute-start.4 = (f32[25,8,128]{2,1,0:T(8,128)S(1)}, f32[25,8,128]{2,1,0:T(8,128)S(1)}, u32[]{:S(2)}, u32[]{:S(2)}) collective-permute-start(f32[25,8,128]{2,1,0:T(8,128)S(1)} %get-tuple-element.38), channel_id=1, source_target_pairs={{0,2},{1,3},{2,0},{3,1},{4,6},{5,7},{6,4},{7,5},{8,10},{9,11},{10,... | collective-permute-start | bytes 307208 | tf_op jit(solution)/shard_map/ppermute | solution.py:438
  44.8 10.1 %collective-permute-start.5 = (f32[25,8,128]{2,1,0:T(8,128)S(1)}, f32[25,8,128]{2,1,0:T(8,128)S(1)}, u32[]{:S(2)}, u32[]{:S(2)}) collective-permute-start(f32[25,8,128]{2,1,0:T(8,128)S(1)} %get-tuple-element.39), channel_id=1, source_target_pairs={{0,3},{1,2},{2,1},{3,0},{4,7},{5,6},{6,5},{7,4},{8,11},{9,10},{10,... | collective-permute-start | bytes 307208 | tf_op jit(solution)/shard_map/ppermute | solution.py:438
  54.9 4.9 %copy-start.2 = (f32[1,128,128]{2,1,0:T(8,128)S(1)}, f32[1,128,128]{2,1,0:T(8,128)}, u32[]{:S(2)}) copy-start(f32[1,128,128]{2,1,0:T(8,128)} %cols_ref.1) | copy-start | bytes 196612
  55.0 7.8 %collective-permute-start.6 = (f32[4,48,128]{2,1,0:T(8,128)S(1)}, f32[4,48,128]{2,1,0:T(8,128)S(1)}, u32[]{:S(2)}, u32[]{:S(2)}) collective-permute-start(f32[4,48,128]{2,1,0:T(8,128)S(1)} %get-tuple-element.42), channel_id=1, source_target_pairs={{0,4},{4,0},{8,12},{12,8},{1,5},{5,1},{9,13},{13,9},{2,6},{6,2},{1... | collective-permute-start | bytes 294920 | tf_op jit(solution)/shard_map/ppermute | solution.py:563
  55.8 11.8 %collective-permute-start.7 = (f32[4,48,128]{2,1,0:T(8,128)S(1)}, f32[4,48,128]{2,1,0:T(8,128)S(1)}, u32[]{:S(2)}, u32[]{:S(2)}) collective-permute-start(f32[4,48,128]{2,1,0:T(8,128)S(1)} %get-tuple-element.43), channel_id=1, source_target_pairs={{0,8},{4,12},{8,0},{12,4},{1,9},{5,13},{9,1},{13,5},{2,10},{6,14},... | collective-permute-start | bytes 294920 | tf_op jit(solution)/shard_map/ppermute | solution.py:563
  59.8 7.9 %collective-permute-start.8 = (f32[4,48,128]{2,1,0:T(8,128)S(1)}, f32[4,48,128]{2,1,0:T(8,128)S(1)}, u32[]{:S(2)}, u32[]{:S(2)}) collective-permute-start(f32[4,48,128]{2,1,0:T(8,128)S(1)} %get-tuple-element.44), channel_id=1, source_target_pairs={{0,12},{4,8},{8,4},{12,0},{1,13},{5,9},{9,5},{13,1},{2,14},{6,10},... | collective-permute-start | bytes 294920 | tf_op jit(solution)/shard_map/ppermute | solution.py:563
  69.6 4.0 %collective-permute-start.10 = (f32[4,16,128]{2,1,0:T(8,128)S(1)}, f32[4,16,128]{2,1,0:T(8,128)S(1)}, u32[]{:S(2)}, u32[]{:S(2)}) collective-permute-start(f32[4,16,128]{2,1,0:T(8,128)S(1)} %get-tuple-element.49.refs_0_), channel_id=1, source_target_pairs={{0,2},{1,3},{2,0},{3,1},{4,6},{5,7},{6,4},{7,5},{8,10},{9,11},{10,... | collective-permute-start | bytes 98312 | tf_op jit(solution)/shard_map/ppermute | solution.py:438
  71.2 3.3 %collective-permute-start.11 = (f32[4,16,128]{2,1,0:T(8,128)S(1)}, f32[4,16,128]{2,1,0:T(8,128)S(1)}, u32[]{:S(2)}, u32[]{:S(2)}) collective-permute-start(f32[4,16,128]{2,1,0:T(8,128)S(1)} %get-tuple-element.50), channel_id=1, source_target_pairs={{0,3},{1,2},{2,1},{3,0},{4,7},{5,6},{6,5},{7,4},{8,11},{9,10},{10,... | collective-permute-start | bytes 98312 | tf_op jit(solution)/shard_map/ppermute | solution.py:438
  71.2 3.3 %collective-permute-start.9 = (f32[4,16,128]{2,1,0:T(8,128)S(1)}, f32[4,16,128]{2,1,0:T(8,128)S(1)}, u32[]{:S(2)}, u32[]{:S(2)}) collective-permute-start(f32[4,16,128]{2,1,0:T(8,128)S(1)} %get-tuple-element.50), channel_id=1, source_target_pairs={{0,1},{1,0},{2,3},{3,2},{4,5},{5,4},{6,7},{7,6},{8,9},{9,8},{10,11... | collective-permute-start | bytes 98312 | tf_op jit(solution)/shard_map/ppermute | solution.py:438
